TPU v7x, 512 devices: a whole 4x4x16 slice. The times are simulated.
512 devices in a mesh: lat: 16 (over x_lo, y, core), lon: 32 (over x_hi, z).
Axes of the slice: x: 4 (x_hi: 2, x_lo: 2; x = x_hi * 2 + x_lo), y: 4, z: 16, core: 2. Of those that a mesh axis runs over, the one named last changes fastest.
Arguments:
- field: float32 [256, 16, 4096], P(None, 'lat', 'lon'), may hold values from -6 to 6
- cotangent: float32 [256, 16, 4096], P(None, 'lat', 'lon'), may hold values from -6 to 6
- conv_weight: float32 [3, 3, 256, 256], replicated, may hold values from -0.125 to 0.125
- spectral_filter: float32 [2, 256, 4096], P(None, None, 'lon'), may hold values from -6 to 6
Outputs:
- output: float32 [256, 16, 4096], P(None, 'lat', 'lon')
- input_grad: float32 [256, 16, 4096], P(None, 'lat', 'lon')
- filter_grad: float32 [2, 256, 4096], P(None, None, 'lon')
All inputs are finite; a program needn't handle non-finite values.
Results may differ from a plain program's by a relative error of at most 0.00014.
Values sent between devices are 32-bit elements; how exact they have to be, the bound alone decides.
A program may use at most 64 MiB of HBM per device.

v0:
```python
import jax
import jax.numpy as jnp
from jax import lax
from jax.sharding import PartitionSpec as P

precise = lax.Precision.HIGHEST


def padded_2(array, sides, width, wrap):
    for axis, dim in sides:
        peers, length = (lax.axis_size(axis), array.shape[dim])
        up = [(i, (i + 1) % peers) for i in range(peers if wrap else peers - 1)]
        down = [(j, i) for i, j in up]
        last = lax.slice_in_dim(array, length - width, length, axis=dim)
        leading = lax.slice_in_dim(array, 0, width, axis=dim)
        before = lax.ppermute(last, axis, up)
        after = lax.ppermute(leading, axis, down)
        array = jnp.concatenate([before, array, after], axis=dim)
    return array


def partner(array, axis, stride):
    return lax.ppermute(array, axis, [(i, i ^ 1 << stride) for i in range(lax.axis_size(axis))])


def angle_table(first, second, modulus):
    product = first[:, None] * second[None, :] % modulus
    return 2.0 * jnp.pi / modulus * product.astype(jnp.float32)


def apply_taps(padded, taps, lat_rows, columns):
    total = jnp.zeros((taps.shape[2], lat_rows, columns), jnp.float32)
    for tap_row in range(3):
        for tap_col in range(3):
            window = padded[:, tap_row : tap_row + lat_rows, tap_col : tap_col + columns]
            total = total + jnp.einsum(
                "oi,iab->oab", taps[tap_row, tap_col], window, precision=precise
            )
    return total


def with_rims(field):
    wider = padded_2(field, (("lon", 2),), 1, True)
    return padded_2(wider, (("lat", 1),), 1, False)


def local_forward(real_part, imag_part):
    columns = real_part.shape[-1]
    places = lax.iota(jnp.int32, columns)
    angles = angle_table(places, places, columns)
    cosine = jnp.cos(angles)
    sine = jnp.sin(angles)
    out_real = jnp.dot(real_part, cosine, precision=precise) + jnp.dot(
        imag_part, sine, precision=precise
    )
    out_imag = jnp.dot(imag_part, cosine, precision=precise) - jnp.dot(
        real_part, sine, precision=precise
    )
    return (out_real, out_imag)


def local_inverse(real_part, imag_part):
    columns = real_part.shape[-1]
    places = lax.iota(jnp.int32, columns)
    angles = angle_table(places, places, columns)
    cosine = jnp.cos(angles)
    sine = jnp.sin(angles)
    out_real = jnp.dot(real_part, cosine, precision=precise) - jnp.dot(
        imag_part, sine, precision=precise
    )
    out_imag = jnp.dot(imag_part, cosine, precision=precise) + jnp.dot(
        real_part, sine, precision=precise
    )
    return (out_real / columns, out_imag / columns)


def section_angles(place, bit_pos, columns):
    offsets = lax.iota(jnp.int32, columns)
    start = place % 2**bit_pos * columns
    span = 2 * columns * 2**bit_pos
    angles = 2.0 * jnp.pi / span * (start + offsets).astype(jnp.float32)
    upper = place // 2**bit_pos % 2 == 1
    return (jnp.cos(angles), jnp.sin(angles), upper)


def forward_pairs(field):
    extent = lax.axis_size("lon")
    width_bits = extent.bit_length() - 1
    place = lax.axis_index("lon")
    columns = field.shape[-1]
    data = jnp.stack([field, jnp.zeros_like(field)])
    for bit_pos in reversed(range(width_bits)):
        other = partner(data, "lon", bit_pos)
        cosine, sine, upper = section_angles(place, bit_pos, columns)
        differ = other - data
        turned = jnp.stack(
            [differ[0] * cosine + differ[1] * sine, differ[1] * cosine - differ[0] * sine]
        )
        data = jnp.where(upper, turned, data + other)
    out_real, out_imag = local_forward(data[0], data[1])
    return jnp.stack([out_real, out_imag])


def inverse_pairs(spectrum):
    extent = lax.axis_size("lon")
    width_bits = extent.bit_length() - 1
    place = lax.axis_index("lon")
    columns = spectrum.shape[-1]
    back_real, back_imag = local_inverse(spectrum[0], spectrum[1])
    data = jnp.stack([back_real, back_imag])
    for bit_pos in range(width_bits):
        cosine, sine, upper = section_angles(place, bit_pos, columns)
        turned = jnp.stack([data[0] * cosine - data[1] * sine, data[1] * cosine + data[0] * sine])
        outgoing = jnp.where(upper, turned, data)
        other = partner(outgoing, "lon", bit_pos)
        data = jnp.where(upper, other - outgoing, outgoing + other) * 0.5
    return data[0]


def on_device(field, cotangent, conv_weight, spectral_filter):
    lat_rows = field.shape[1]
    columns = field.shape[2]
    total_len = columns * lax.axis_size("lon")
    mixed = apply_taps(with_rims(field), conv_weight, lat_rows, columns)
    hidden_spec = forward_pairs(mixed)
    cot_spec = forward_pairs(cotangent)
    gain_real = spectral_filter[0][:, None, :]
    gain_imag = spectral_filter[1][:, None, :]
    filtered = jnp.stack(
        [
            gain_real * hidden_spec[0] - gain_imag * hidden_spec[1],
            gain_real * hidden_spec[1] + gain_imag * hidden_spec[0],
        ]
    )
    adjoint = jnp.stack(
        [
            gain_real * cot_spec[0] + gain_imag * cot_spec[1],
            gain_real * cot_spec[1] - gain_imag * cot_spec[0],
        ]
    )
    shaped = inverse_pairs(filtered)
    back_field = inverse_pairs(adjoint)
    output = field + shaped
    local_grad = (
        jnp.stack(
            [
                jnp.sum(hidden_spec[0] * cot_spec[0] + hidden_spec[1] * cot_spec[1], axis=1),
                jnp.sum(hidden_spec[0] * cot_spec[1] - hidden_spec[1] * cot_spec[0], axis=1),
            ]
        )
        / total_len
    )
    filter_grad = lax.psum(local_grad, "lat")
    flipped_taps = jnp.transpose(conv_weight[::-1, ::-1], (0, 1, 3, 2))
    input_grad = cotangent + apply_taps(with_rims(back_field), flipped_taps, lat_rows, columns)
    return (output, input_grad, filter_grad)


def solution(mesh):
    placed = (P(None, "lat", "lon"), P(None, "lat", "lon"), P(), P(None, None, "lon"))
    return jax.shard_map(
        on_device,
        mesh=mesh,
        in_specs=placed,
        out_specs=(P(None, "lat", "lon"), P(None, "lat", "lon"), P(None, None, "lon")),
        check_vma=False,
    )
```

profile of v0, /device:TPU:1, one launch (start us, length us, event | category | flops | bytes accessed | tf_op | source)
XLA Modules:
  0.0 503.1 jit_solution(4956193246249797645)
XLA Ops:
  7.2 1.5 fusion.168
  8.7 4.4 collective-permute-start
  13.1 12.0 %collective-permute-start.1 = (f32[256,1,1]{2,1,0:T(1,128)S(1)}, f32[256,1,1]{2,1,0:T(1,128)S(1)}, u32[]{:S(2)}, u32[]{:S(2)}) collective-permute-start(f32[256,1,1]{2,1,0:T(1,128)S(1)} %get-tuple-element.71), channel_id=1, source_target_pairs={{1,0},{2,1},{3,2},{4,3},{5,4},{6,5},{7,6},{8,7},{9,8},{10,9},{11,1... | collective-permute-start | bytes 3080 | tf_op jit(solution)/shard_map/ppermute | solution.py:17
  26.1 2.1 collective-permute-start.14
  28.2 1.8 pad_maximum_fusion
  30.0 3.1 collective-permute-start.3
  33.2 3.1 collective-permute-start.2
  36.3 1.9 pad_maximum_fusion.4
  43.8 4.6 collective-permute-start.4
  48.6 6.7 %collective-permute-done.4 = f32[2,256,1,128]{1,3,2,0:T(8,128)S(1)} collective-permute-done((f32[2,256,1,128]{1,3,2,0:T(8,128)}, f32[2,256,1,128]{1,3,2,0:T(8,128)S(1)}, u32[]{:S(2)}, u32[]{:S(2)}) %collective-permute-start.4) | collective-permute-done | bytes 262176 | tf_op jit(solution)/shard_map/ppermute | solution.py:23
  56.4 9.2 %collective-permute-start.5 = (f32[2,256,1,128]{1,3,2,0:T(8,128)}, f32[2,256,1,128]{1,3,2,0:T(8,128)}, u32[]{:S(2)}, u32[]{:S(2)}) collective-permute-start(f32[2,256,1,128]{1,3,2,0:T(8,128)} %maximum_select_fusion), channel_id=1, source_target_pairs={{0,8},{1,9},{2,10},{3,11},{4,12},{5,13},{6,14},{7,15},{8,0},{9,1},... | collective-permute-start | bytes 786440 | tf_op jit(solution)/shard_map/ppermute | solution.py:23
  66.4 4.8 collective-permute-start.15
  71.2 20.3 %collective-permute-done.5 = f32[2,256,1,128]{1,3,2,0:T(8,128)} collective-permute-done((f32[2,256,1,128]{1,3,2,0:T(8,128)}, f32[2,256,1,128]{1,3,2,0:T(8,128)}, u32[]{:S(2)}, u32[]{:S(2)}) %collective-permute-start.5) | collective-permute-done | bytes 262176 | tf_op jit(solution)/shard_map/ppermute | solution.py:23
  91.5 1.0 fusion.190
  92.5 20.8 %collective-permute-done.15 = f32[2,256,1,128]{1,3,2,0:T(8,128)} collective-permute-done((f32[2,256,1,128]{1,3,2,0:T(8,128)}, f32[2,256,1,128]{1,3,2,0:T(8,128)}, u32[]{:S(2)}, u32[]{:S(2)}) %collective-permute-start.15) | collective-permute-done | bytes 262176 | tf_op jit(solution)/shard_map/ppermute | solution.py:23
  113.3 1.1 fusion.191
  114.6 1.0 maximum_select_fusion.11
  115.6 1.9 collective-permute-start.16
  117.6 1.1 maximum_select_fusion.1
  118.7 7.3 %collective-permute-start.6 = (f32[2,256,1,128]{1,3,2,0:T(8,128)S(1)}, f32[2,256,1,128]{1,3,2,0:T(8,128)}, u32[]{:S(2)}, u32[]{:S(2)}) collective-permute-start(f32[2,256,1,128]{1,3,2,0:T(8,128)S(1)} %maximum_select_fusion.1), channel_id=1, source_target_pairs={{0,4},{1,5},{2,6},{3,7},{4,0},{5,1},{6,2},{7,3},{8,12},{9,13},{10,... | collective-permute-start | bytes 786440 | tf_op jit(solution)/shard_map/ppermute | solution.py:23
  126.1 30.2 %collective-permute-done.16 = f32[2,256,1,128]{1,3,2,0:T(8,128)} collective-permute-done((f32[2,256,1,128]{1,3,2,0:T(8,128)S(1)}, f32[2,256,1,128]{1,3,2,0:T(8,128)}, u32[]{:S(2)}, u32[]{:S(2)}) %collective-permute-start.16) | collective-permute-done | bytes 262176 | tf_op jit(solution)/shard_map/ppermute | solution.py:23
  157.3 4.6 collective-permute-done.6
  163.0 1.0 maximum_select_fusion.12
  164.0 1.9 collective-permute-start.17
  165.9 1.0 maximum_select_fusion.2
  167.0 4.3 collective-permute-start.7
  171.3 10.2 %collective-permute-done.17 = f32[2,256,1,128]{1,3,2,0:T(8,128)} collective-permute-done((f32[2,256,1,128]{1,3,2,0:T(8,128)S(1)}, f32[2,256,1,128]{1,3,2,0:T(8,128)}, u32[]{:S(2)}, u32[]{:S(2)}) %collective-permute-start.17) | collective-permute-done | bytes 262176 | tf_op jit(solution)/shard_map/ppermute | solution.py:23
  182.5 4.6 collective-permute-done.7
  188.3 1.0 maximum_select_fusion.13
  189.3 1.9 collective-permute-start.18
  192.2 3.5 collective-permute-start.8
  195.9 2.8 collective-permute-done.18
  199.6 4.5 collective-permute-done.8
  204.4 1.0 maximum_select_fusion.14
  209.4 1.3 add_bitcast_fusion
  215.2 2.2 collective-permute-start.19
  217.5 3.0 collective-permute-start.9
  220.6 3.0 collective-permute-done.19
  223.6 5.6 %collective-permute-done.9 = f32[2,256,1,128]{1,3,2,0:T(8,128)S(1)} collective-permute-done((f32[2,256,1,128]{1,3,2,0:T(8,128)S(1)}, f32[2,256,1,128]{1,3,2,0:T(8,128)S(1)}, u32[]{:S(2)}, u32[]{:S(2)}) %collective-permute-start.9) | collective-permute-done | bytes 262176 | tf_op jit(solution)/shard_map/ppermute | solution.py:23
  229.5 1.9 collective-permute-start.10
  231.5 4.3 collective-permute-start.20
  235.7 15.6 %collective-permute-done.10 = f32[2,256,1,128]{1,3,2,0:T(8,128)S(1)} collective-permute-done((f32[2,256,1,128]{1,3,2,0:T(8,128)S(1)}, f32[2,256,1,128]{1,3,2,0:T(8,128)S(1)}, u32[]{:S(2)}, u32[]{:S(2)}) %collective-permute-start.10) | collective-permute-done | bytes 262176 | tf_op jit(solution)/shard_map/ppermute | solution.py:23
  251.4 5.6 %collective-permute-done.20 = f32[2,256,1,128]{1,3,2,0:T(8,128)S(1)} collective-permute-done((f32[2,256,1,128]{1,3,2,0:T(8,128)S(1)}, f32[2,256,1,128]{1,3,2,0:T(8,128)S(1)}, u32[]{:S(2)}, u32[]{:S(2)}) %collective-permute-start.20) | collective-permute-done | bytes 262176 | tf_op jit(solution)/shard_map/ppermute | solution.py:23
  257.2 3.8 collective-permute-start.11
  261.1 5.4 %collective-permute-start.21 = (f32[2,256,1,128]{1,3,2,0:T(8,128)S(1)}, f32[2,256,1,128]{1,3,2,0:T(8,128)S(1)}, u32[]{:S(2)}, u32[]{:S(2)}) collective-permute-start(f32[2,256,1,128]{1,3,2,0:T(8,128)S(1)} %maximum_select_fusion.17), channel_id=1, source_target_pairs={{0,4},{1,5},{2,6},{3,7},{4,0},{5,1},{6,2},{7,3},{8,12},{9,13},{10,... | collective-permute-start | bytes 786440 | tf_op jit(solution)/shard_map/ppermute | solution.py:23
  266.4 35.6 %collective-permute-done.11 = f32[2,256,1,128]{1,3,2,0:T(8,128)S(1)} collective-permute-done((f32[2,256,1,128]{1,3,2,0:T(8,128)S(1)}, f32[2,256,1,128]{1,3,2,0:T(8,128)S(1)}, u32[]{:S(2)}, u32[]{:S(2)}) %collective-permute-start.11) | collective-permute-done | bytes 262176 | tf_op jit(solution)/shard_map/ppermute | solution.py:23
  302.1 16.9 %collective-permute-done.21 = f32[2,256,1,128]{1,3,2,0:T(8,128)S(1)} collective-permute-done((f32[2,256,1,128]{1,3,2,0:T(8,128)S(1)}, f32[2,256,1,128]{1,3,2,0:T(8,128)S(1)}, u32[]{:S(2)}, u32[]{:S(2)}) %collective-permute-start.21) | collective-permute-done | bytes 262176 | tf_op jit(solution)/shard_map/ppermute | solution.py:23
  320.6 10.3 %collective-permute-start.12 = (f32[2,256,1,128]{1,3,2,0:T(8,128)}, f32[2,256,1,128]{1,3,2,0:T(8,128)}, u32[]{:S(2)}, u32[]{:S(2)}) collective-permute-start(f32[2,256,1,128]{1,3,2,0:T(8,128)} %maximum_select_fusion.8), channel_id=1, source_target_pairs={{0,8},{1,9},{2,10},{3,11},{4,12},{5,13},{6,14},{7,15},{8,0},{9,1},... | collective-permute-start | bytes 786440 | tf_op jit(solution)/shard_map/ppermute | solution.py:23
  331.6 3.7 collective-permute-start.22
  335.3 1.6 reverse_bitcast_fusion
  337.7 4.7 collective-permute-done.12
  342.5 1.1 select_multiply_fusion.4
  343.6 6.0 %collective-permute-done.22 = f32[2,256,1,128]{1,3,2,0:T(8,128)} collective-permute-done((f32[2,256,1,128]{1,3,2,0:T(8,128)}, f32[2,256,1,128]{1,3,2,0:T(8,128)}, u32[]{:S(2)}, u32[]{:S(2)}) %collective-permute-start.22) | collective-permute-done | bytes 262176 | tf_op jit(solution)/shard_map/ppermute | solution.py:23
  350.8 1.9 collective-permute-start.23
  353.5 4.9 collective-permute-start.13
  358.4 1.9 collective-permute-done.23
  361.2 1.9 collective-permute-start.24
  363.1 8.9 %collective-permute-start.25 = (f32[256,1,1]{0,2,1:T(1,128)S(1)}, f32[256,1,1]{0,2,1:T(1,128)S(1)}, u32[]{:S(2)}, u32[]{:S(2)}) collective-permute-start(f32[256,1,1]{0,2,1:T(1,128)S(1)} %get-tuple-element.63), channel_id=1, source_target_pairs={{1,0},{2,1},{3,2},{4,3},{5,4},{6,5},{7,6},{8,7},{9,8},{10,9},{11,1... | collective-permute-start | bytes 3080 | tf_op jit(solution)/shard_map/ppermute | solution.py:17
  372.0 1.2 fusion.19
  374.0 5.7 %collective-permute-start.27 = (f32[256,1,130]{0,2,1:T(8,128)S(1)}, f32[256,1,130]{0,2,1:T(8,128)S(1)}, u32[]{:S(2)}, u32[]{:S(2)}) collective-permute-start(f32[256,1,130]{0,2,1:T(8,128)S(1)} %pad_maximum_fusion.1), channel_id=1, source_target_pairs={{32,0},{64,32},{96,64},{128,96},{160,128},{192,160},{224,192},{256... | collective-permute-start | bytes 399368 | tf_op jit(solution)/shard_map/ppermute | solution.py:17
  379.7 1.9 collective-permute-start.26
  382.6 1.1 collective-permute-done.26
  386.0 108.6 %all-reduce.4.cloned.1.call-done = f32[2,256,128]{2,1,0:T(8,128)} async-done(((f32[2,256,128]{2,1,0:T(8,128)}), f32[2,256,128]{2,1,0:T(8,128)}) %all-reduce.4.cloned.1.call-update) | async-done | bytes 262160 | tf_op jit(solution)/shard_map/psum | solution.py:153
  494.6 1.7 copy.23
  (146 shorter events, 34.2 us)
Async XLA Ops:
  7.2 31.0 %copy-start = (f32[3,3,256,256]{3,2,1,0:T(8,128)S(1)}, f32[3,3,256,256]{3,2,1,0:T(8,128)}, u32[]{:S(2)}) copy-start(f32[3,3,256,256]{3,2,1,0:T(8,128)} %param.6) | copy-start | bytes 7077892
  7.2 487.4 %all-reduce.4.cloned.1.call-start = ((), (), s32[]{:S(2)}) async-start(), calls=%async_computation | async-start | bytes 524288 | tf_op jit(solution)/shard_map/psum | solution.py:153
  8.7 19.5 %collective-permute-start = (f32[256,1,1]{2,1,0:T(1,128)S(1)}, f32[256,1,1]{2,1,0:T(1,128)S(1)}, u32[]{:S(2)}, u32[]{:S(2)}) collective-permute-start(f32[256,1,1]{2,1,0:T(1,128)S(1)} %get-tuple-element.70), channel_id=1, source_target_pairs={{0,1},{1,2},{2,3},{3,4},{4,5},{5,6},{6,7},{7,8},{8,9},{9,10},{10,1... | collective-permute-start | bytes 3080 | tf_op jit(solution)/shard_map/ppermute | solution.py:16
  13.1 15.2 %collective-permute-start.1 = (f32[256,1,1]{2,1,0:T(1,128)S(1)}, f32[256,1,1]{2,1,0:T(1,128)S(1)}, u32[]{:S(2)}, u32[]{:S(2)}) collective-permute-start(f32[256,1,1]{2,1,0:T(1,128)S(1)} %get-tuple-element.71), channel_id=1, source_target_pairs={{1,0},{2,1},{3,2},{4,3},{5,4},{6,5},{7,6},{8,7},{9,8},{10,9},{11,1... | collective-permute-start | bytes 3080 | tf_op jit(solution)/shard_map/ppermute | solution.py:17
  26.1 22.5 %collective-permute-start.14 = (f32[2,256,1,128]{1,3,2,0:T(8,128)S(1)}, f32[2,256,1,128]{1,3,2,0:T(8,128)S(1)}, u32[]{:S(2)}, u32[]{:S(2)}) collective-permute-start(f32[2,256,1,128]{1,3,2,0:T(8,128)S(1)} %stack.165), channel_id=1, source_target_pairs={{0,16},{1,17},{2,18},{3,19},{4,20},{5,21},{6,22},{7,23},{8,24},{9,... | collective-permute-start | bytes 786440 | tf_op jit(solution)/shard_map/ppermute | solution.py:23
  30.0 8.6 %collective-permute-start.3 = (f32[256,1,130]{2,1,0:T(1,128)S(1)}, f32[256,1,130]{2,1,0:T(1,128)S(1)}, u32[]{:S(2)}, u32[]{:S(2)}) collective-permute-start(f32[256,1,130]{2,1,0:T(1,128)S(1)} %pad_maximum_fusion), channel_id=1, source_target_pairs={{32,0},{64,32},{96,64},{128,96},{160,128},{192,160},{224,192},{256... | collective-permute-start | bytes 399368 | tf_op jit(solution)/shard_map/ppermute | solution.py:17
  33.2 6.4 %collective-permute-start.2 = (f32[256,1,130]{2,1,0:T(1,128)S(1)}, f32[256,1,130]{2,1,0:T(1,128)S(1)}, u32[]{:S(2)}, u32[]{:S(2)}) collective-permute-start(f32[256,1,130]{2,1,0:T(1,128)S(1)} %pad_maximum_fusion), channel_id=1, source_target_pairs={{0,32},{32,64},{64,96},{96,128},{128,160},{160,192},{192,224},{224... | collective-permute-start | bytes 399368 | tf_op jit(solution)/shard_map/ppermute | solution.py:16
  38.1 3.3 copy-start.2
  43.8 11.5 %collective-permute-start.4 = (f32[2,256,1,128]{1,3,2,0:T(8,128)}, f32[2,256,1,128]{1,3,2,0:T(8,128)S(1)}, u32[]{:S(2)}, u32[]{:S(2)}) collective-permute-start(f32[2,256,1,128]{1,3,2,0:T(8,128)} %stack.148), channel_id=1, source_target_pairs={{0,16},{1,17},{2,18},{3,19},{4,20},{5,21},{6,22},{7,23},{8,24},{9,... | collective-permute-start | bytes 786440 | tf_op jit(solution)/shard_map/ppermute | solution.py:23
  55.5 10.1 %copy-start.5 = (f32[1,256,1,128]{1,3,2,0:T(8,128)}, f32[1,256,1,128]{1,3,2,0:T(8,128)S(1)}, u32[]{:S(2)}) copy-start(f32[1,256,1,128]{1,3,2,0:T(8,128)S(1)} %get-tuple-element.30) | copy-start | bytes 393220
  55.5 10.9 %copy-start.7 = (f32[1,256,1,128]{1,3,2,0:T(8,128)}, f32[1,256,1,128]{1,3,2,0:T(8,128)S(1)}, u32[]{:S(2)}) copy-start(f32[1,256,1,128]{1,3,2,0:T(8,128)S(1)} %get-tuple-element.31) | copy-start | bytes 393220
  55.5 59.1 %copy-start.3 = (f32[1,256,1,128]{1,3,2,0:T(8,128)}, f32[1,256,1,128]{1,3,2,0:T(8,128)S(1)}, u32[]{:S(2)}) copy-start(f32[1,256,1,128]{1,3,2,0:T(8,128)S(1)} %get-tuple-element.92) | copy-start | bytes 393220
  55.5 59.1 %copy-start.4 = (f32[1,256,1,128]{1,3,2,0:T(8,128)}, f32[1,256,1,128]{1,3,2,0:T(8,128)S(1)}, u32[]{:S(2)}) copy-start(f32[1,256,1,128]{1,3,2,0:T(8,128)S(1)} %get-tuple-element.93) | copy-start | bytes 393220
  56.4 35.1 %collective-permute-start.5 = (f32[2,256,1,128]{1,3,2,0:T(8,128)}, f32[2,256,1,128]{1,3,2,0:T(8,128)}, u32[]{:S(2)}, u32[]{:S(2)}) collective-permute-start(f32[2,256,1,128]{1,3,2,0:T(8,128)} %maximum_select_fusion), channel_id=1, source_target_pairs={{0,8},{1,9},{2,10},{3,11},{4,12},{5,13},{6,14},{7,15},{8,0},{9,1},... | collective-permute-start | bytes 786440 | tf_op jit(solution)/shard_map/ppermute | solution.py:23
  66.4 46.9 %collective-permute-start.15 = (f32[2,256,1,128]{1,3,2,0:T(8,128)}, f32[2,256,1,128]{1,3,2,0:T(8,128)}, u32[]{:S(2)}, u32[]{:S(2)}) collective-permute-start(f32[2,256,1,128]{1,3,2,0:T(8,128)} %maximum_select_fusion.10), channel_id=1, source_target_pairs={{0,8},{1,9},{2,10},{3,11},{4,12},{5,13},{6,14},{7,15},{8,0},{9,1},... | collective-permute-start | bytes 786440 | tf_op jit(solution)/shard_map/ppermute | solution.py:23
  71.2 43.4 %copy-start.6 = (f32[1,256,1,128]{1,3,2,0:T(8,128)S(1)}, f32[1,256,1,128]{1,3,2,0:T(8,128)}, u32[]{:S(2)}) copy-start(f32[1,256,1,128]{1,3,2,0:T(8,128)} %copy-done.5) | copy-start | bytes 393220
  71.2 43.4 %copy-start.8 = (f32[1,256,1,128]{1,3,2,0:T(8,128)S(1)}, f32[1,256,1,128]{1,3,2,0:T(8,128)}, u32[]{:S(2)}) copy-start(f32[1,256,1,128]{1,3,2,0:T(8,128)} %copy-done.7) | copy-start | bytes 393220
  115.6 40.6 %collective-permute-start.16 = (f32[2,256,1,128]{1,3,2,0:T(8,128)S(1)}, f32[2,256,1,128]{1,3,2,0:T(8,128)}, u32[]{:S(2)}, u32[]{:S(2)}) collective-permute-start(f32[2,256,1,128]{1,3,2,0:T(8,128)S(1)} %maximum_select_fusion.11), channel_id=1, source_target_pairs={{0,4},{1,5},{2,6},{3,7},{4,0},{5,1},{6,2},{7,3},{8,12},{9,13},{10,... | collective-permute-start | bytes 786440 | tf_op jit(solution)/shard_map/ppermute | solution.py:23
  118.7 43.2 %collective-permute-start.6 = (f32[2,256,1,128]{1,3,2,0:T(8,128)S(1)}, f32[2,256,1,128]{1,3,2,0:T(8,128)}, u32[]{:S(2)}, u32[]{:S(2)}) collective-permute-start(f32[2,256,1,128]{1,3,2,0:T(8,128)S(1)} %maximum_select_fusion.1), channel_id=1, source_target_pairs={{0,4},{1,5},{2,6},{3,7},{4,0},{5,1},{6,2},{7,3},{8,12},{9,13},{10,... | collective-permute-start | bytes 786440 | tf_op jit(solution)/shard_map/ppermute | solution.py:23
  126.0 40.9 %copy-start.15 = (f32[128]{0:T(128)}, f32[128]{0:T(128)S(1)}, u32[]{:S(2)}) copy-start(f32[128]{0:T(128)S(1)} %get-tuple-element.98) | copy-start | bytes 1540
  126.1 40.9 %copy-start.17 = (f32[128]{0:T(128)}, f32[128]{0:T(128)S(1)}, u32[]{:S(2)}) copy-start(f32[128]{0:T(128)S(1)} %get-tuple-element.99) | copy-start | bytes 1540
  164.0 17.5 %collective-permute-start.17 = (f32[2,256,1,128]{1,3,2,0:T(8,128)S(1)}, f32[2,256,1,128]{1,3,2,0:T(8,128)}, u32[]{:S(2)}, u32[]{:S(2)}) collective-permute-start(f32[2,256,1,128]{1,3,2,0:T(8,128)S(1)} %maximum_select_fusion.12), channel_id=1, source_target_pairs={{0,2},{1,3},{2,0},{3,1},{4,6},{5,7},{6,4},{7,5},{8,10},{9,11},{10,... | collective-permute-start | bytes 786440 | tf_op jit(solution)/shard_map/ppermute | solution.py:23
  167.0 20.2 %collective-permute-start.7 = (f32[2,256,1,128]{1,3,2,0:T(8,128)S(1)}, f32[2,256,1,128]{1,3,2,0:T(8,128)}, u32[]{:S(2)}, u32[]{:S(2)}) collective-permute-start(f32[2,256,1,128]{1,3,2,0:T(8,128)S(1)} %maximum_select_fusion.2), channel_id=1, source_target_pairs={{0,2},{1,3},{2,0},{3,1},{4,6},{5,7},{6,4},{7,5},{8,10},{9,11},{10,... | collective-permute-start | bytes 786440 | tf_op jit(solution)/shard_map/ppermute | solution.py:23
  171.3 20.9 %copy-start.19 = (f32[128]{0:T(128)}, f32[128]{0:T(128)S(1)}, u32[]{:S(2)}) copy-start(f32[128]{0:T(128)S(1)} %get-tuple-element.100) | copy-start | bytes 1540
  171.3 20.9 %copy-start.21 = (f32[128]{0:T(128)}, f32[128]{0:T(128)S(1)}, u32[]{:S(2)}) copy-start(f32[128]{0:T(128)S(1)} %get-tuple-element.101) | copy-start | bytes 1540
  189.3 9.4 %collective-permute-start.18 = (f32[2,256,1,128]{1,3,2,0:T(8,128)S(1)}, f32[2,256,1,128]{1,3,2,0:T(8,128)}, u32[]{:S(2)}, u32[]{:S(2)}) collective-permute-start(f32[2,256,1,128]{1,3,2,0:T(8,128)S(1)} %maximum_select_fusion.13), channel_id=1, source_target_pairs={{0,1},{1,0},{2,3},{3,2},{4,5},{5,4},{6,7},{7,6},{8,9},{9,8},{10,11... | collective-permute-start | bytes 786440 | tf_op jit(solution)/shard_map/ppermute | solution.py:23
  192.2 11.9 %collective-permute-start.8 = (f32[2,256,1,128]{1,3,2,0:T(8,128)S(1)}, f32[2,256,1,128]{1,3,2,0:T(8,128)S(1)}, u32[]{:S(2)}, u32[]{:S(2)}) collective-permute-start(f32[2,256,1,128]{1,3,2,0:T(8,128)S(1)} %maximum_select_fusion.3), channel_id=1, source_target_pairs={{0,1},{1,0},{2,3},{3,2},{4,5},{5,4},{6,7},{7,6},{8,9},{9,8},{10,11... | collective-permute-start | bytes 786440 | tf_op jit(solution)/shard_map/ppermute | solution.py:23
  204.3 5.1 %copy-start.14 = (f32[2,256,128]{2,1,0:T(8,128)S(1)}, f32[2,256,128]{2,1,0:T(8,128)}, u32[]{:S(2)}) copy-start(f32[2,256,128]{2,1,0:T(8,128)} %param.7) | copy-start | bytes 786436
  214.6 14.7 %copy-start.20 = (f32[128]{0:T(128)S(1)}, f32[128]{0:T(128)}, u32[]{:S(2)}) copy-start(f32[128]{0:T(128)} %copy-done.19) | copy-start | bytes 1540
  214.6 14.7 %copy-start.22 = (f32[128]{0:T(128)S(1)}, f32[128]{0:T(128)}, u32[]{:S(2)}) copy-start(f32[128]{0:T(128)} %copy-done.21) | copy-start | bytes 1540
  215.2 8.4 %collective-permute-start.19 = (f32[2,256,1,128]{1,3,2,0:T(8,128)S(1)}, f32[2,256,1,128]{1,3,2,0:T(8,128)S(1)}, u32[]{:S(2)}, u32[]{:S(2)}) collective-permute-start(f32[2,256,1,128]{1,3,2,0:T(8,128)S(1)} %maximum_select_fusion.15), channel_id=1, source_target_pairs={{0,1},{1,0},{2,3},{3,2},{4,5},{5,4},{6,7},{7,6},{8,9},{9,8},{10,11... | collective-permute-start | bytes 786440 | tf_op jit(solution)/shard_map/ppermute | solution.py:23
  217.5 11.7 %collective-permute-start.9 = (f32[2,256,1,128]{1,3,2,0:T(8,128)S(1)}, f32[2,256,1,128]{1,3,2,0:T(8,128)S(1)}, u32[]{:S(2)}, u32[]{:S(2)}) collective-permute-start(f32[2,256,1,128]{1,3,2,0:T(8,128)S(1)} %maximum_select_fusion.5), channel_id=1, source_target_pairs={{0,1},{1,0},{2,3},{3,2},{4,5},{5,4},{6,7},{7,6},{8,9},{9,8},{10,11... | collective-permute-start | bytes 786440 | tf_op jit(solution)/shard_map/ppermute | solution.py:23
  229.3 27.7 %copy-start.16 = (f32[128]{0:T(128)S(1)}, f32[128]{0:T(128)}, u32[]{:S(2)}) copy-start(f32[128]{0:T(128)} %copy-done.15) | copy-start | bytes 1540
  229.3 27.7 %copy-start.18 = (f32[128]{0:T(128)S(1)}, f32[128]{0:T(128)}, u32[]{:S(2)}) copy-start(f32[128]{0:T(128)} %copy-done.17) | copy-start | bytes 1540
  229.5 21.8 %collective-permute-start.10 = (f32[2,256,1,128]{1,3,2,0:T(8,128)S(1)}, f32[2,256,1,128]{1,3,2,0:T(8,128)S(1)}, u32[]{:S(2)}, u32[]{:S(2)}) collective-permute-start(f32[2,256,1,128]{1,3,2,0:T(8,128)S(1)} %maximum_select_fusion.6), channel_id=1, source_target_pairs={{0,2},{1,3},{2,0},{3,1},{4,6},{5,7},{6,4},{7,5},{8,10},{9,11},{10,... | collective-permute-start | bytes 786440 | tf_op jit(solution)/shard_map/ppermute | solution.py:23
  231.5 25.5 %collective-permute-start.20 = (f32[2,256,1,128]{1,3,2,0:T(8,128)S(1)}, f32[2,256,1,128]{1,3,2,0:T(8,128)S(1)}, u32[]{:S(2)}, u32[]{:S(2)}) collective-permute-start(f32[2,256,1,128]{1,3,2,0:T(8,128)S(1)} %maximum_select_fusion.16), channel_id=1, source_target_pairs={{0,2},{1,3},{2,0},{3,1},{4,6},{5,7},{6,4},{7,5},{8,10},{9,11},{10,... | collective-permute-start | bytes 786440 | tf_op jit(solution)/shard_map/ppermute | solution.py:23
  257.2 44.8 %collective-permute-start.11 = (f32[2,256,1,128]{1,3,2,0:T(8,128)S(1)}, f32[2,256,1,128]{1,3,2,0:T(8,128)S(1)}, u32[]{:S(2)}, u32[]{:S(2)}) collective-permute-start(f32[2,256,1,128]{1,3,2,0:T(8,128)S(1)} %maximum_select_fusion.7), channel_id=1, source_target_pairs={{0,4},{1,5},{2,6},{3,7},{4,0},{5,1},{6,2},{7,3},{8,12},{9,13},{10,... | collective-permute-start | bytes 786440 | tf_op jit(solution)/shard_map/ppermute | solution.py:23
  261.1 57.9 %collective-permute-start.21 = (f32[2,256,1,128]{1,3,2,0:T(8,128)S(1)}, f32[2,256,1,128]{1,3,2,0:T(8,128)S(1)}, u32[]{:S(2)}, u32[]{:S(2)}) collective-permute-start(f32[2,256,1,128]{1,3,2,0:T(8,128)S(1)} %maximum_select_fusion.17), channel_id=1, source_target_pairs={{0,4},{1,5},{2,6},{3,7},{4,0},{5,1},{6,2},{7,3},{8,12},{9,13},{10,... | collective-permute-start | bytes 786440 | tf_op jit(solution)/shard_map/ppermute | solution.py:23
  319.2 0.7 copy-start.10
  319.2 17.8 %copy-start.9 = (f32[1,256,1,128]{1,3,2,0:T(8,128)}, f32[1,256,1,128]{1,3,2,0:T(8,128)S(1)}, u32[]{:S(2)}) copy-start(f32[1,256,1,128]{1,3,2,0:T(8,128)S(1)} %get-tuple-element.78) | copy-start | bytes 393220
  320.6 21.9 %collective-permute-start.12 = (f32[2,256,1,128]{1,3,2,0:T(8,128)}, f32[2,256,1,128]{1,3,2,0:T(8,128)}, u32[]{:S(2)}, u32[]{:S(2)}) collective-permute-start(f32[2,256,1,128]{1,3,2,0:T(8,128)} %maximum_select_fusion.8), channel_id=1, source_target_pairs={{0,8},{1,9},{2,10},{3,11},{4,12},{5,13},{6,14},{7,15},{8,0},{9,1},... | collective-permute-start | bytes 786440 | tf_op jit(solution)/shard_map/ppermute | solution.py:23
  331.6 18.0 %collective-permute-start.22 = (f32[2,256,1,128]{1,3,2,0:T(8,128)}, f32[2,256,1,128]{1,3,2,0:T(8,128)}, u32[]{:S(2)}, u32[]{:S(2)}) collective-permute-start(f32[2,256,1,128]{1,3,2,0:T(8,128)} %maximum_select_fusion.18), channel_id=1, source_target_pairs={{0,8},{1,9},{2,10},{3,11},{4,12},{5,13},{6,14},{7,15},{8,0},{9,1},... | collective-permute-start | bytes 786440 | tf_op jit(solution)/shard_map/ppermute | solution.py:23
  337.7 15.0 %copy-start.12 = (f32[1,256,128]{2,1,0:T(8,128)S(1)}, f32[1,256,128]{2,1,0:T(8,128)}, u32[]{:S(2)}) copy-start(f32[1,256,128]{2,1,0:T(8,128)} %get-tuple-element.6) | copy-start | bytes 393220
  337.7 15.0 %copy-start.13 = (f32[1,256,128]{2,1,0:T(8,128)S(1)}, f32[1,256,128]{2,1,0:T(8,128)}, u32[]{:S(2)}) copy-start(f32[1,256,128]{2,1,0:T(8,128)} %get-tuple-element.7) | copy-start | bytes 393220
  343.6 28.4 %copy-start.1 = (f32[3,3,256,256]{2,3,1,0:T(8,128)S(1)}, f32[3,3,256,256]{2,3,1,0:T(8,128)}, u32[]{:S(2)}) copy-start(f32[3,3,256,256]{2,3,1,0:T(8,128)} %reverse_bitcast_fusion) | copy-start | bytes 7077892
  350.6 22.6 %copy-start.11 = (f32[256,1,128]{0,2,1:T(8,128)S(1)}, f32[256,1,128]{0,2,1:T(8,128)}, u32[]{:S(2)}) copy-start(f32[256,1,128]{0,2,1:T(8,128)} %copy.12) | copy-start | bytes 393220
  350.8 9.5 %collective-permute-start.23 = (f32[2,256,1,128]{1,3,2,0:T(8,128)S(1)}, f32[2,256,1,128]{1,3,2,0:T(8,128)}, u32[]{:S(2)}, u32[]{:S(2)}) collective-permute-start(f32[2,256,1,128]{1,3,2,0:T(8,128)S(1)} %maximum_select_fusion.19), channel_id=1, source_target_pairs={{0,16},{1,17},{2,18},{3,19},{4,20},{5,21},{6,22},{7,23},{8,24},{9,... | collective-permute-start | bytes 786440 | tf_op jit(solution)/shard_map/ppermute | solution.py:23
  353.5 19.7 %collective-permute-start.13 = (f32[2,256,1,128]{1,3,2,0:T(8,128)S(1)}, f32[2,256,1,128]{1,3,2,0:T(8,128)S(1)}, u32[]{:S(2)}, u32[]{:S(2)}) collective-permute-start(f32[2,256,1,128]{1,3,2,0:T(8,128)S(1)} %maximum_select_fusion.9), channel_id=1, source_target_pairs={{0,16},{1,17},{2,18},{3,19},{4,20},{5,21},{6,22},{7,23},{8,24},{9,... | collective-permute-start | bytes 786440 | tf_op jit(solution)/shard_map/ppermute | solution.py:23
  361.2 12.8 %collective-permute-start.24 = (f32[256,1,1]{0,2,1:T(1,128)S(1)}, f32[256,1,1]{0,2,1:T(1,128)S(1)}, u32[]{:S(2)}, u32[]{:S(2)}) collective-permute-start(f32[256,1,1]{0,2,1:T(1,128)S(1)} %get-tuple-element.62), channel_id=1, source_target_pairs={{0,1},{1,2},{2,3},{3,4},{4,5},{5,6},{6,7},{7,8},{8,9},{9,10},{10,1... | collective-permute-start | bytes 3080 | tf_op jit(solution)/shard_map/ppermute | solution.py:16
  363.1 10.9 %collective-permute-start.25 = (f32[256,1,1]{0,2,1:T(1,128)S(1)}, f32[256,1,1]{0,2,1:T(1,128)S(1)}, u32[]{:S(2)}, u32[]{:S(2)}) collective-permute-start(f32[256,1,1]{0,2,1:T(1,128)S(1)} %get-tuple-element.63), channel_id=1, source_target_pairs={{1,0},{2,1},{3,2},{4,3},{5,4},{6,5},{7,6},{8,7},{9,8},{10,9},{11,1... | collective-permute-start | bytes 3080 | tf_op jit(solution)/shard_map/ppermute | solution.py:17
  374.0 7.9 %collective-permute-start.27 = (f32[256,1,130]{0,2,1:T(8,128)S(1)}, f32[256,1,130]{0,2,1:T(8,128)S(1)}, u32[]{:S(2)}, u32[]{:S(2)}) collective-permute-start(f32[256,1,130]{0,2,1:T(8,128)S(1)} %pad_maximum_fusion.1), channel_id=1, source_target_pairs={{32,0},{64,32},{96,64},{128,96},{160,128},{192,160},{224,192},{256... | collective-permute-start | bytes 399368 | tf_op jit(solution)/shard_map/ppermute | solution.py:17
  379.7 4.0 collective-permute-start.26
Sparse Core Ops, SparseCore 0:
  353.6 140.9 all-reduce.3
where the time goes:
time: 505 us; the launch traced here: 503 us
  waiting for transfers between devices  309 us (61%)
  starting transfers between devices  124 us (25%)
  other arithmetic  27 us (5%)
  matrix products  16.7 us (3%)
  between operations  15.3 us (3%)
  local copies, waits for them, and re-layouts  10.8 us (2%)
    ppermute x20, waiting for transfers between devices, partner(): lax.ppermute(array, axis, [(i, i ^ 1 << stride) for i in range(lax.axis_s...  200 us
    psum x1, waiting for transfers between devices, on_device(): filter_grad = lax.psum(local_grad, 'lat')  109 us
    ppermute x20, starting transfers between devices, partner(): lax.ppermute(array, axis, [(i, i ^ 1 << stride) for i in range(lax.axis_s...  83 us
    ppermute x4, starting transfers between devices, padded_2(): after = lax.ppermute(leading, axis, down)  29.6 us
    ppermute x4, starting transfers between devices, padded_2(): before = lax.ppermute(last, axis, up)  11.3 us
  transfers between devices with their start and end apart: 29, of which 20 were waited for; matrix products, arithmetic and copies ran while one was open for 6% of the time, Pallas kernels for 0%

commit v1 on v0

v1 whole, which is shorter than its diff:
```python
import functools
import math

import jax
import jax.numpy as jnp
import ml_dtypes
import numpy as np
from jax import lax
from jax.experimental import pallas as pl
from jax.experimental.pallas import tpu as pltpu
from jax.sharding import PartitionSpec as P

MESH = pl.DeviceIdType.MESH
f32, bf16 = jnp.float32, jnp.bfloat16


def split(value):
    high = value.astype(bf16)
    return high, (value - high.astype(f32)).astype(bf16)


def matmul(lhs, rhs, dims):
    return lax.dot_general(lhs, rhs, (dims, ((), ())), preferred_element_type=f32)


def turn(value, angle):
    re, im = value
    c, s = math.cos(angle), math.sin(angle)
    return re * c - im * s, im * c + re * s


def conj(value):
    return value[0], None if value[1] is None else -value[1]


def plus(a, b):
    if a[1] is None or b[1] is None:
        return a[0] + b[0], a[1] if b[1] is None else b[1]
    return a[0] + b[0], a[1] + b[1]


def minus(a, b):
    if a[1] is None or b[1] is None:
        return a[0] - b[0], a[1] if b[1] is None else -b[1]
    return a[0] - b[0], a[1] - b[1]


def real_forward(xs):
    n = len(xs)
    if n == 1:
        return [(xs[0], None)]
    if n == 2:
        return [(xs[0] + xs[1], None), (xs[0] - xs[1], None)]
    even, odd = real_forward(xs[0::2]), real_forward(xs[1::2])
    out = [None] * (n // 2 + 1)
    for r in range(n // 4 + 1):
        e, o = even[r], odd[r]
        if r == 0:
            out[0], out[n // 2] = (e[0] + o[0], None), (e[0] - o[0], None)
        elif r == n // 4:
            out[r] = (e[0], -o[0])
        else:
            o = turn(o, -2 * math.pi * r / n)
            out[r], out[n // 2 - r] = plus(e, o), conj(minus(e, o))
    return out


def real_inverse(spec):
    n = 2 * (len(spec) - 1)
    if n == 2:
        a, b = spec[0][0], spec[1][0]
        return [a + b, a - b]
    even, odd = [None] * (n // 4 + 1), [None] * (n // 4 + 1)
    for r in range(n // 4 + 1):
        a, b = spec[r], spec[n // 2 - r]
        if r == 0:
            even[0], odd[0] = (a[0] + b[0], None), (a[0] - b[0], None)
        elif r == n // 4:
            even[r], odd[r] = (2.0 * a[0], None), (-2.0 * a[1], None)
        else:
            b = conj(b)
            even[r], odd[r] = plus(a, b), turn(minus(a, b), 2 * math.pi * r / n)
    out = [None] * n
    out[0::2], out[1::2] = real_inverse(even), real_inverse(odd)
    return out


def flipped_bits(place, extent):
    width = extent.bit_length() - 1
    return sum((place >> bit & 1) << (width - 1 - bit) for bit in range(width))


def tables(lats, lons, columns):
    groups = lons // lats
    residues = [flipped_bits(slot % groups * lats + slot // groups, lons) for slot in range(lons)]
    m = np.arange(columns)
    inner = 2 * np.pi * (np.outer(m, m) % columns) / columns
    c, s = np.cos(inner), np.sin(inner)
    forward = np.block([[c, -s], [s, c]])
    inverse = np.block([[c, s], [-s, c]]) / (columns * lons)
    mats = []
    for mat in (forward, inverse):
        high = mat.astype(np.float32).astype(ml_dtypes.bfloat16)
        mats += [high, (mat - high.astype(np.float64)).astype(ml_dtypes.bfloat16)]
    outer = 2 * np.pi * np.outer(residues, m) / (columns * lons)
    twiddle = np.stack([np.cos(outer), np.sin(outer)]).astype(np.float32)
    return residues, np.stack(mats), twiddle


def layer_kernel(
    lats, lons, residues,
    field, cot, weight, gain, mats, twiddle,
    out, igrad, fgrad,
    wbuf, wrow_hi, wrow_lo, wcol_hi, wcol_lo, xe, be, windows,
    mixed, cot_line, mix_line, back_send, shape_send, back, shaped,
    lhs, cspec, gpart, gbuf, pbuf, rsbuf, fsum, fgpart, fgbuf,
    wsem, halo_send, halo_recv, a2a_send, a2a_recv,
    gp_send, gp_recv, ga_send, ga_recv, rs_send, rs_recv, fp_send, fp_recv, fa_send, fa_recv,
):
    a, d = lax.axis_index("lat"), lax.axis_index("lon")
    groups = lons // lats
    cols = field.shape[2]
    chans = lons * 8
    up, down = lax.rem(a + 1, lats), lax.rem(a + lats - 1, lats)
    east, west = lax.rem(d + 1, lons), lax.rem(d + lons - 1, lons)

    barrier = pltpu.get_barrier_semaphore()

    def greet(lat, lon):
        pl.semaphore_signal(barrier, inc=1, device_id=(lat, lon), device_id_type=MESH)

    def greet_lat(i, carry):
        greet(lax.rem(a + i, lats), d)
        return carry

    def greet_lon(i, carry):
        greet(a, lax.rem(d + i, lons))
        return carry

    lax.fori_loop(1, lats, greet_lat, 0)
    for lat in (up, down):
        for lon in (east, west):
            greet(lat, lon)
    lax.fori_loop(1, lons, greet_lon, 0)

    def send(src, dst, send_sem, recv_sem, lat, lon):
        copy = pltpu.make_async_remote_copy(
            src_ref=src, dst_ref=dst, send_sem=send_sem, recv_sem=recv_sem,
            device_id=(lat, lon), device_id_type=MESH,
        )
        copy.start()

    def await_bytes(ref, sem):
        pltpu.make_async_copy(ref, ref, sem).wait()

    def exchange(src, dst, index):
        def step(i, carry):
            peer = lax.rem(d + i, lons)
            send(src.at[peer], dst.at[d], a2a_send.at[index], a2a_recv.at[index], a, peer)
            return carry

        lax.fori_loop(1, lons, step, 0)

    def exchanged(src, dst, index):
        await_bytes(dst.at[pl.ds(0, lons - 1)], a2a_recv.at[index])
        dst[d] = src[d]

    def exchange_sent(src, index):
        await_bytes(src.at[pl.ds(0, lons - 1)], a2a_send.at[index])

    low, high = pl.ds(0, 8), pl.ds(cols + 8, 8)
    middle = pl.ds(8, cols)
    rows = [(up, 0), (down, 2)]
    edges = [(up, 0), (a, 1), (down, 2)]

    def halo_plan(ext, index):
        plan = []
        for lat, slot in rows:
            plan.append((ext.at[1, middle], ext.at[slot, middle], lat, d))
        for lat, slot in edges:
            plan.append((ext.at[1, pl.ds(8, 8)], ext.at[slot, high], lat, west))
            plan.append((ext.at[1, pl.ds(cols, 8)], ext.at[slot, low], lat, east))
        return [
            pltpu.make_async_remote_copy(
                src_ref=src, dst_ref=dst, send_sem=halo_send.at[index, i],
                recv_sem=halo_recv.at[index, i], device_id=(lat, lon), device_id_type=MESH,
            )
            for i, (src, dst, lat, lon) in enumerate(plan)
        ]

    wcopy = pltpu.make_async_copy(weight, wbuf, wsem)
    wcopy.start()
    xe[1, middle] = field[...].reshape(chans, cols).T

    pl.semaphore_wait(barrier, lats - 1 + lons - 1 + 4)

    field_halo = halo_plan(xe, 0)
    for copy in field_halo:
        copy.start()

    for h in range(groups):
        e = lax.rem(d + lats - a, lats) + lats * h

        @pl.when(e != d)
        def _():
            send(gain.at[:, e], gpart.at[d // lats], gp_send.at[h], gp_recv.at[d // lats], a, e)

        @pl.when(e == d)
        def _():
            gpart[d // lats] = gain[:, e]

    exchange(cot, cot_line, 0)

    wcopy.wait()
    for t in range(9):
        w_hi, w_lo = split(wbuf[t])
        block = slice(t * chans, (t + 1) * chans)
        wrow_hi[:, block] = w_hi
        wrow_lo[:, block] = w_lo
        wcol_hi[block, :] = w_hi
        wcol_lo[block, :] = w_lo

    gain_slot = lax.rem(a + d, lats)
    for g in range(groups):
        @pl.when(gain_slot + lats * g != d)
        def _():
            await_bytes(gpart.at[g], gp_recv.at[g])

    def gather_gain(i, carry):
        send(gpart, gbuf.at[gain_slot], ga_send, ga_recv, lax.rem(a + i, lats), d)
        return carry

    lax.fori_loop(1, lats, gather_gain, 0)

    def fill_windows(ext, backward):
        for slot in range(3):
            for s in range(3):
                t = (2 - slot if backward else slot) * 3 + s
                start = 9 - s if backward else 7 + s
                window = ext[slot, start : start + cols, :]
                if slot == 0:
                    window = jnp.where(a > 0, window, 0.0)
                if slot == 2:
                    window = jnp.where(a < lats - 1, window, 0.0)
                w_hi, w_lo = split(window)
                block = slice(t * chans, (t + 1) * chans)
                windows[0:cols, block] = w_hi
                windows[cols : 2 * cols, block] = w_lo

    for copy in field_halo:
        copy.wait_recv()
    fill_windows(xe, False)
    both = matmul(wrow_hi[...], windows[...], ((1,), (1,)))
    small = matmul(wrow_lo[...], windows[0:cols, :], ((1,), (1,)))
    mixed[...] = (both[:, :cols] + both[:, cols:] + small).reshape(lons, 8, cols)
    exchange(mixed, mix_line, 1)

    def transform(line):
        spec = real_forward([line[i] for i in range(lons)])
        for slot, r in enumerate(residues):
            re, im = spec[r] if 2 * r <= lons else conj(spec[lons - r])
            c, s = twiddle[0, slot : slot + 1, :], twiddle[1, slot : slot + 1, :]
            block = slice(slot * 8, slot * 8 + 8)
            if im is None:
                lhs[block, 0:cols] = re * c
                lhs[block, cols : 2 * cols] = -re * s
            else:
                lhs[block, 0:cols] = re * c + im * s
                lhs[block, cols : 2 * cols] = im * c - re * s
        hi, lo = split(lhs[...])
        dims = ((1,), (0,))
        full = matmul(hi, mats[0], dims) + matmul(hi, mats[1], dims) + matmul(lo, mats[0], dims)
        return full[:, :cols], full[:, cols:]

    def untransform(re, im, dst):
        hi, lo = split(jnp.concatenate([re, im], axis=1))
        dims = ((1,), (0,))
        lhs[...] = matmul(hi, mats[2], dims) + matmul(hi, mats[3], dims) + matmul(lo, mats[2], dims)
        turned = [None] * lons
        for slot, r in enumerate(residues):
            block = slice(slot * 8, slot * 8 + 8)
            c, s = twiddle[0, slot : slot + 1, :], twiddle[1, slot : slot + 1, :]
            re, im = lhs[block, 0:cols], lhs[block, cols : 2 * cols]
            turned[r] = (re * c - im * s, im * c + re * s)
        half = [(turned[0][0], None)]
        for r in range(1, lons // 2):
            half.append(tuple(0.5 * v for v in plus(turned[r], conj(turned[lons - r]))))
        half.append((turned[lons // 2][0], None))
        for i, value in enumerate(real_inverse(half)):
            dst[i] = value

    exchanged(cot, cot_line, 0)
    c_re, c_im = transform(cot_line)
    cspec[0] = c_re
    cspec[1] = c_im
    await_bytes(gbuf.at[pl.ds(0, lats - 1)], ga_recv)
    gbuf[gain_slot] = gpart[...]
    g_re = gbuf[:, :, 0].reshape(chans, cols)
    g_im = gbuf[:, :, 1].reshape(chans, cols)
    untransform(g_re * c_re + g_im * c_im, g_re * c_im - g_im * c_re, back_send)
    exchange(back_send, back, 2)

    exchanged(mixed, mix_line, 1)
    s_re, s_im = transform(mix_line)
    c_re, c_im = cspec[0], cspec[1]
    scale = 1.0 / (cols * lons)
    tiles = (lats, groups, 8, cols)
    pbuf[:, :, 0] = ((s_re * c_re + s_im * c_im) * scale).reshape(tiles)
    pbuf[:, :, 1] = ((s_re * c_im - s_im * c_re) * scale).reshape(tiles)

    def scatter_sums(i, carry):
        peer = lax.rem(a + i, lats)
        send(pbuf.at[lax.rem(peer + d, lats)], rsbuf.at[a], rs_send, rs_recv, peer, d)
        return carry

    lax.fori_loop(1, lats, scatter_sums, 0)

    g_re = gbuf[:, :, 0].reshape(chans, cols)
    g_im = gbuf[:, :, 1].reshape(chans, cols)
    untransform(g_re * s_re - g_im * s_im, g_re * s_im + g_im * s_re, shape_send)
    exchange(shape_send, shaped, 3)

    await_bytes(rsbuf.at[pl.ds(0, lats - 1)], rs_recv)
    rsbuf[a] = pbuf[gain_slot]
    fsum[...] = jnp.sum(rsbuf[...], axis=0)
    for h in range(groups):
        e = gain_slot + lats * h

        @pl.when(e != d)
        def _():
            send(fsum.at[h], fgpart.at[d // lats], fp_send.at[h], fp_recv.at[d // lats], a, e)

        @pl.when(e == d)
        def _():
            fgpart[d // lats] = fsum[h]

    exchanged(back_send, back, 2)
    be[1, middle] = back[...].reshape(chans, cols).T
    back_halo = halo_plan(be, 1)
    for copy in back_halo:
        copy.start()

    sum_slot = lax.rem(d + lats - a, lats)
    for g in range(groups):
        @pl.when(sum_slot + lats * g != d)
        def _():
            await_bytes(fgpart.at[g], fp_recv.at[g])

    def gather_sums(i, carry):
        send(fgpart, fgbuf.at[sum_slot], fa_send, fa_recv, lax.rem(a + i, lats), d)
        return carry

    lax.fori_loop(1, lats, gather_sums, 0)

    for copy in back_halo:
        copy.wait_recv()
    fill_windows(be, True)
    both = matmul(windows[...], wcol_hi[...], ((1,), (0,)))
    small = matmul(windows[0:cols, :], wcol_lo[...], ((1,), (0,)))
    grad = (both[:cols] + both[cols:] + small).T
    igrad[...] = cot[...] + grad.reshape(lons, 8, cols)

    await_bytes(fgbuf.at[pl.ds(0, lats - 1)], fa_recv)
    fgbuf[sum_slot] = fgpart[...]
    for i in range(lons):
        fgrad[:, i] = fgbuf[i % lats, i // lats]

    exchanged(shape_send, shaped, 3)
    out[...] = field[...] + shaped[...]

    for copy in field_halo + back_halo:
        copy.wait_send()
    for h in range(groups):
        @pl.when(lax.rem(d + lats - a, lats) + lats * h != d)
        def _():
            await_bytes(gpart.at[h], gp_send.at[h])

        @pl.when(gain_slot + lats * h != d)
        def _():
            await_bytes(fsum.at[h], fp_send.at[h])

    await_bytes(gbuf.at[pl.ds(0, lats - 1)], ga_send)
    await_bytes(rsbuf.at[pl.ds(0, lats - 1)], rs_send)
    await_bytes(fgbuf.at[pl.ds(0, lats - 1)], fa_send)
    for index, src in enumerate((cot, mixed, back_send, shape_send)):
        exchange_sent(src, index)


def solution(mesh):
    lats, lons = mesh.shape["lat"], mesh.shape["lon"]
    groups = lons // lats

    def on_device(field, cotangent, conv_weight, spectral_filter):
        chans, _, cols = field.shape
        residues, mats, twiddle = tables(lats, lons, cols)
        tiles = (lons, 8, cols)
        tile = jax.ShapeDtypeStruct(tiles, f32)
        vmem = pl.BlockSpec(memory_space=pltpu.VMEM)
        line = pltpu.VMEM(tiles, f32)
        dma = pltpu.SemaphoreType.DMA
        share = (groups, 2, 8, cols)
        shares = (lats,) + share
        out, igrad, fgrad = pl.pallas_call(
            functools.partial(layer_kernel, lats, lons, residues),
            out_shape=(tile, tile, jax.ShapeDtypeStruct((2,) + tiles, f32)),
            in_specs=[vmem, vmem, pl.BlockSpec(memory_space=pl.ANY), vmem, vmem, vmem],
            out_specs=(vmem, vmem, vmem),
            scratch_shapes=[
                pltpu.VMEM((9, chans, chans), f32),
                pltpu.VMEM((chans, 9 * chans), bf16),
                pltpu.VMEM((chans, 9 * chans), bf16),
                pltpu.VMEM((9 * chans, chans), bf16),
                pltpu.VMEM((9 * chans, chans), bf16),
                pltpu.VMEM((3, cols + 16, chans), f32),
                pltpu.VMEM((3, cols + 16, chans), f32),
                pltpu.VMEM((2 * cols, 9 * chans), bf16),
                line, line, line, line, line, line, line,
                pltpu.VMEM((chans, 2 * cols), f32),
                pltpu.VMEM((2, chans, cols), f32),
                pltpu.VMEM(share, f32),
                pltpu.VMEM(shares, f32),
                pltpu.VMEM(shares, f32),
                pltpu.VMEM(shares, f32),
                pltpu.VMEM(share, f32),
                pltpu.VMEM(share, f32),
                pltpu.VMEM(shares, f32),
                dma, dma((2, 8)), dma((2, 8)), dma((4,)), dma((4,)),
                dma((groups,)), dma((groups,)), dma, dma, dma, dma,
                dma((groups,)), dma((groups,)), dma, dma,
            ],
            compiler_params=pltpu.CompilerParams(
                collective_id=0, has_side_effects=True, vmem_limit_bytes=48 << 20
            ),
        )(
            field.reshape(tiles),
            cotangent.reshape(tiles),
            conv_weight.reshape(9, chans, chans),
            spectral_filter.reshape((2,) + tiles),
            jnp.asarray(mats),
            jnp.asarray(twiddle),
        )
        shape = (chans, 1, cols)
        return out.reshape(shape), igrad.reshape(shape), fgrad.reshape(2, chans, cols)

    placed = (P(None, "lat", "lon"), P(None, "lat", "lon"), P(), P(None, None, "lon"))
    return jax.shard_map(
        on_device,
        mesh=mesh,
        in_specs=placed,
        out_specs=(P(None, "lat", "lon"), P(None, "lat", "lon"), P(None, None, "lon")),
        check_vma=False,
    )
```

time: 505 us -> 68 us (0.13)
  waiting for transfers between devices: 309 us -> 0 us
  starting transfers between devices: 124 us -> 0 us
  Pallas kernels: 0 us -> 58.8 us
  other arithmetic: 27 us -> 0 us
  matrix products: 16.7 us -> 0 us
  between operations: 15.3 us -> 0.65 us
    ppermute x28 -> x0, waiting for transfers between devices: 201 us -> none  [the longest x20 200 us: partner(): lax.ppermute(array, axis, [(i, i ^ 1 << stride) for i in range(lax.axis_s...]
    ppermute x28 -> x0, starting transfers between devices: 124 us -> none  [the longest x20 83 us: partner(): lax.ppermute(array, axis, [(i, i ^ 1 << stride) for i in range(lax.axis_s...]
    psum x1 -> x0, waiting for transfers between devices: 109 us -> none  [on_device(): filter_grad = lax.psum(local_grad, 'lat')]
    pallas_call x0 -> x1, Pallas kernels: none -> 58.8 us  [on_device(): pl.pallas_call(functools.partial(layer_kernel, lats, lons, residues), out...]
    dot_general x34 -> x0, matrix products: 16.7 us -> none  [the longest x18 7.11 us: apply_taps(): jnp.einsum('oi,iab->oab', taps[tap_row, tap_col], window, precision=precise)]
    select_n x20 -> x0, other arithmetic: 10.7 us -> none  [the longest x10 8.91 us: forward_pairs(): data = jnp.where(upper, turned, data + other)]
    sub x14 -> x0, other arithmetic: 7.64 us -> none  [the longest x10 7.12 us: forward_pairs(): differ = other - data]
  transfers between devices with their start and end apart: 29 -> 0, of which waited for: 20 -> 0; matrix products, arithmetic and copies ran while one was open for 6% -> 0% of each run, Pallas kernels for 0% -> 0%
where the time goes in v1:
time: 68 us; the launch traced here: 67.7 us
  Pallas kernels  58.8 us (86%)
  local copies, waits for them, and re-layouts  8.23 us (12%)
    pallas_call x1, Pallas kernels, on_device(): pl.pallas_call(functools.partial(layer_kernel, lats, lons, residues), out...  58.8 us
    unnamed x15, local copies, waits for them, and re-layouts  8.23 us

profile of v1, /device:TPU:1, one launch (start us, length us, event | category | flops | bytes accessed | tf_op | source)
XLA Modules:
  0.0 67.7 jit_solution(1006328925040814135)
XLA Ops:
  0.6 0.0 copy-start
  0.6 1.7 %copy-done = f32[3,3,256,256]{3,2,1,0:T(8,128)S(1)} copy-done((f32[3,3,256,256]{3,2,1,0:T(8,128)S(1)}, f32[3,3,256,256]{3,2,1,0:T(8,128)}, u32[]{:S(2)}) %copy-start) | copy-done | bytes 2359320
  2.3 0.0 copy-start.1
  2.3 1.0 %copy-done.1 = bf16[4,256,256]{2,1,0:T(8,128)(2,1)S(1)} copy-done((bf16[4,256,256]{2,1,0:T(8,128)(2,1)S(1)}, bf16[4,256,256]{2,1,0:T(8,128)(2,1)}, u32[]{:S(2)}) %copy-start.1) | copy-done | bytes 524312
  3.3 0.0 copy-start.2
  3.3 0.9 %copy-done.2 = f32[2,256,128]{2,1,0:T(8,128)S(1)} copy-done((f32[2,256,128]{2,1,0:T(8,128)S(1)}, f32[2,256,128]{2,1,0:T(8,128)}, u32[]{:S(2)}) %copy-start.2) | copy-done | bytes 262168
  4.3 0.0 copy-start.3
  4.3 0.9 %copy-done.3 = f32[256,1,128]{2,1,0:T(1,128)S(1)} copy-done((f32[256,1,128]{2,1,0:T(1,128)S(1)}, f32[256,1,128]{2,1,0:T(1,128)}, u32[]{:S(2)}) %copy-start.3) | copy-done | bytes 131096
  5.2 0.0 copy-start.4
  5.2 0.9 %copy-done.4 = f32[256,1,128]{2,1,0:T(1,128)S(1)} copy-done((f32[256,1,128]{2,1,0:T(1,128)S(1)}, f32[256,1,128]{2,1,0:T(1,128)}, u32[]{:S(2)}) %copy-start.4) | copy-done | bytes 131096
  6.1 0.0 copy-start.5
  6.1 0.8 %copy-done.5 = f32[2,32,128]{2,1,0:T(8,128)S(1)} copy-done((f32[2,32,128]{2,1,0:T(8,128)S(1)}, f32[2,32,128]{2,1,0:T(8,128)}, u32[]{:S(2)}) %copy-start.5) | copy-done | bytes 32792
  6.9 58.8 %shard_map.85 = (f32[32,8,128]{2,1,0:T(8,128)S(1)}, f32[32,8,128]{2,1,0:T(8,128)S(1)}, f32[2,32,8,128]{3,2,1,0:T(8,128)S(1)}) custom-call(f32[32,8,128]{2,1,0:T(8,128)S(1)} %bitcast.16, f32[32,8,128]{2,1,0:T(8,128)S(1)} %bitcast.17, f32[9,256,256]{2,1,0:T(8,128)S(1)} %bitcast.11, f32[2,32,8,128]{3,2,1,0:T(8,128)S(1)} %bitcast.13, ...), custom_call_target="tpu_custom_call" | custom-call | tf_op jit(solution)/shard_map/pallas_call | solution.py:403
  65.7 0.7 copy.14
  66.3 0.7 copy.15
  67.0 0.7 %copy.16 = f32[2,256,128]{2,1,0:T(8,128)} copy(f32[2,256,128]{2,1,0:T(8,128)S(1)} %bitcast.12) | data formatting | bytes 524288
Async XLA Ops:
  0.6 1.7 %copy-start = (f32[3,3,256,256]{3,2,1,0:T(8,128)S(1)}, f32[3,3,256,256]{3,2,1,0:T(8,128)}, u32[]{:S(2)}) copy-start(f32[3,3,256,256]{3,2,1,0:T(8,128)} %param.8) | copy-start | bytes 7077892
  2.3 1.0 %copy-start.1 = (bf16[4,256,256]{2,1,0:T(8,128)(2,1)S(1)}, bf16[4,256,256]{2,1,0:T(8,128)(2,1)}, u32[]{:S(2)}) copy-start(bf16[4,256,256]{2,1,0:T(8,128)(2,1)} %constant.4.clone.mats) | copy-start | bytes 1572868
  3.3 0.9 %copy-start.2 = (f32[2,256,128]{2,1,0:T(8,128)S(1)}, f32[2,256,128]{2,1,0:T(8,128)}, u32[]{:S(2)}) copy-start(f32[2,256,128]{2,1,0:T(8,128)} %param.9) | copy-start | bytes 786436
  4.3 0.9 %copy-start.3 = (f32[256,1,128]{2,1,0:T(1,128)S(1)}, f32[256,1,128]{2,1,0:T(1,128)}, u32[]{:S(2)}) copy-start(f32[256,1,128]{2,1,0:T(1,128)} %param.6) | copy-start | bytes 393220
  5.2 0.9 %copy-start.4 = (f32[256,1,128]{2,1,0:T(1,128)S(1)}, f32[256,1,128]{2,1,0:T(1,128)}, u32[]{:S(2)}) copy-start(f32[256,1,128]{2,1,0:T(1,128)} %param.7) | copy-start | bytes 393220
  6.1 0.8 %copy-start.5 = (f32[2,32,128]{2,1,0:T(8,128)S(1)}, f32[2,32,128]{2,1,0:T(8,128)}, u32[]{:S(2)}) copy-start(f32[2,32,128]{2,1,0:T(8,128)} %constant.5.clone.twiddle) | copy-start | bytes 98308

commit v2 on v1

--- a/solution.py
+++ b/solution.py
@@ -109,18 +109,34 @@
 
 def layer_kernel(
     lats, lons, residues,
-    field, cot, weight, gain, mats, twiddle,
+    field_in, cot_in, weight_in, gain_in, mats_in, twiddle_in,
     out, igrad, fgrad,
-    wbuf, wrow_hi, wrow_lo, wcol_hi, wcol_lo, xe, be, windows,
+    field, cot, gain, mats, twiddle, wbuf, wrow_hi, wrow_lo, wcol_hi, wcol_lo, xe, be, windows,
     mixed, cot_line, mix_line, back_send, shape_send, back, shaped,
     lhs, cspec, gpart, gbuf, pbuf, rsbuf, fsum, fgpart, fgbuf,
-    wsem, halo_send, halo_recv, a2a_send, a2a_recv,
+    load_sem, halo_send, halo_recv, a2a_send, a2a_recv,
     gp_send, gp_recv, ga_send, ga_recv, rs_send, rs_recv, fp_send, fp_recv, fa_send, fa_recv,
 ):
     a, d = lax.axis_index("lat"), lax.axis_index("lon")
     groups = lons // lats
     cols = field.shape[2]
     chans = lons * 8
+    ring = lons // 2
+
+    loads = [
+        pltpu.make_async_copy(src, dst, load_sem.at[i])
+        for i, (src, dst) in enumerate(
+            [(field_in, field), (cot_in, cot), (gain_in, gain), (weight_in, wbuf), (twiddle_in, twiddle), (mats_in, mats)]
+        )
+    ]
+    for load in loads:
+        load.start()
+
+    def far_first(u):
+        away = ring // 2 - (u + 2) // 4
+        away = jnp.where(lax.rem((u + 2) // 2, 2) == 1, ring - away, away)
+        half = lax.rem(d // ring + 1 - lax.rem(u, 2), 2)
+        return half * ring + lax.rem(d + away, ring)
     up, down = lax.rem(a + 1, lats), lax.rem(a + lats - 1, lats)
     east, west = lax.rem(d + 1, lons), lax.rem(d + lons - 1, lons)
 
@@ -134,14 +150,14 @@
         return carry
 
     def greet_lon(i, carry):
-        greet(a, lax.rem(d + i, lons))
+        greet(a, far_first(i))
         return carry
 
+    lax.fori_loop(0, lons - 1, greet_lon, 0)
     lax.fori_loop(1, lats, greet_lat, 0)
     for lat in (up, down):
         for lon in (east, west):
             greet(lat, lon)
-    lax.fori_loop(1, lons, greet_lon, 0)
 
     def send(src, dst, send_sem, recv_sem, lat, lon):
         copy = pltpu.make_async_remote_copy(
@@ -155,11 +171,11 @@
 
     def exchange(src, dst, index):
         def step(i, carry):
-            peer = lax.rem(d + i, lons)
+            peer = far_first(i)
             send(src.at[peer], dst.at[d], a2a_send.at[index], a2a_recv.at[index], a, peer)
             return carry
 
-        lax.fori_loop(1, lons, step, 0)
+        lax.fori_loop(0, lons - 1, step, 0)
 
     def exchanged(src, dst, index):
         await_bytes(dst.at[pl.ds(0, lons - 1)], a2a_recv.at[index])
@@ -188,30 +204,31 @@
             for i, (src, dst, lat, lon) in enumerate(plan)
         ]
 
-    wcopy = pltpu.make_async_copy(weight, wbuf, wsem)
-    wcopy.start()
+    loads[0].wait()
     xe[1, middle] = field[...].reshape(chans, cols).T
+    loads[1].wait()
+    loads[2].wait()
 
     pl.semaphore_wait(barrier, lats - 1 + lons - 1 + 4)
+
+    for h in range(groups):
+        e = lax.rem(d + lats - a, lats) + lats * h
+
+        @pl.when(e != d)
+        def _():
+            send(gain.at[:, e], gpart.at[d // lats], gp_send.at[h], gp_recv.at[d // lats], a, e)
+
+        @pl.when(e == d)
+        def _():
+            gpart[d // lats] = gain[:, e]
 
     field_halo = halo_plan(xe, 0)
     for copy in field_halo:
         copy.start()
 
-    for h in range(groups):
-        e = lax.rem(d + lats - a, lats) + lats * h
-
-        @pl.when(e != d)
-        def _():
-            send(gain.at[:, e], gpart.at[d // lats], gp_send.at[h], gp_recv.at[d // lats], a, e)
-
-        @pl.when(e == d)
-        def _():
-            gpart[d // lats] = gain[:, e]
-
     exchange(cot, cot_line, 0)
 
-    wcopy.wait()
+    loads[3].wait()
     for t in range(9):
         w_hi, w_lo = split(wbuf[t])
         block = slice(t * chans, (t + 1) * chans)
@@ -220,40 +237,58 @@
         wcol_hi[block, :] = w_hi
         wcol_lo[block, :] = w_lo
 
+    def fill_windows(ext, slot, backward):
+        for s in range(3):
+            t = (2 - slot if backward else slot) * 3 + s
+            start = 9 - s if backward else 7 + s
+            window = ext[slot, start : start + cols, :]
+            if slot == 0:
+                window = jnp.where(a > 0, window, 0.0)
+            if slot == 2:
+                window = jnp.where(a < lats - 1, window, 0.0)
+            w_hi, w_lo = split(window)
+            block = slice(t * chans, (t + 1) * chans)
+            windows[0:cols, block] = w_hi
+            windows[cols : 2 * cols, block] = w_lo
+
+    def halo_arrived(plan, slot):
+        for i in {0: (0, 2, 3), 1: (4, 5), 2: (1, 6, 7)}[slot]:
+            plan[i].wait_recv()
+
+    def taps(slot, backward):
+        first = 2 - slot if backward else slot
+        return slice(first * 3 * chans, (first * 3 + 3) * chans)
+
     gain_slot = lax.rem(a + d, lats)
-    for g in range(groups):
-        @pl.when(gain_slot + lats * g != d)
-        def _():
-            await_bytes(gpart.at[g], gp_recv.at[g])
-
-    def gather_gain(i, carry):
-        send(gpart, gbuf.at[gain_slot], ga_send, ga_recv, lax.rem(a + i, lats), d)
-        return carry
-
-    lax.fori_loop(1, lats, gather_gain, 0)
-
-    def fill_windows(ext, backward):
-        for slot in range(3):
-            for s in range(3):
-                t = (2 - slot if backward else slot) * 3 + s
-                start = 9 - s if backward else 7 + s
-                window = ext[slot, start : start + cols, :]
-                if slot == 0:
-                    window = jnp.where(a > 0, window, 0.0)
-                if slot == 2:
-                    window = jnp.where(a < lats - 1, window, 0.0)
-                w_hi, w_lo = split(window)
-                block = slice(t * chans, (t + 1) * chans)
-                windows[0:cols, block] = w_hi
-                windows[cols : 2 * cols, block] = w_lo
-
-    for copy in field_halo:
-        copy.wait_recv()
-    fill_windows(xe, False)
-    both = matmul(wrow_hi[...], windows[...], ((1,), (1,)))
-    small = matmul(wrow_lo[...], windows[0:cols, :], ((1,), (1,)))
+
+    def forward_gain():
+        for g in range(groups):
+            @pl.when(gain_slot + lats * g != d)
+            def _():
+                await_bytes(gpart.at[g], gp_recv.at[g])
+
+        def gather_gain(i, carry):
+            send(gpart, gbuf.at[gain_slot], ga_send, ga_recv, lax.rem(a + i, lats), d)
+            return carry
+
+        lax.fori_loop(1, lats, gather_gain, 0)
+
+    halves = []
+    for slot in (1, 0, 2):
+        halo_arrived(field_halo, slot)
+        fill_windows(xe, slot, False)
+        block = taps(slot, False)
+        halves.append(
+            (
+                matmul(wrow_hi[:, block], windows[:, block], ((1,), (1,))),
+                matmul(wrow_lo[:, block], windows[0:cols, block], ((1,), (1,))),
+            )
+        )
+    both = halves[0][0] + halves[1][0] + halves[2][0]
+    small = halves[0][1] + halves[1][1] + halves[2][1]
     mixed[...] = (both[:, :cols] + both[:, cols:] + small).reshape(lons, 8, cols)
     exchange(mixed, mix_line, 1)
+    forward_gain()
 
     def transform(line):
         spec = real_forward([line[i] for i in range(lons)])
@@ -289,6 +324,8 @@
         for i, value in enumerate(real_inverse(half)):
             dst[i] = value
 
+    loads[4].wait()
+    loads[5].wait()
     exchanged(cot, cot_line, 0)
     c_re, c_im = transform(cot_line)
     cspec[0] = c_re
@@ -341,32 +378,44 @@
         copy.start()
 
     sum_slot = lax.rem(d + lats - a, lats)
-    for g in range(groups):
-        @pl.when(sum_slot + lats * g != d)
-        def _():
-            await_bytes(fgpart.at[g], fp_recv.at[g])
-
-    def gather_sums(i, carry):
-        send(fgpart, fgbuf.at[sum_slot], fa_send, fa_recv, lax.rem(a + i, lats), d)
-        return carry
-
-    lax.fori_loop(1, lats, gather_sums, 0)
-
-    for copy in back_halo:
-        copy.wait_recv()
-    fill_windows(be, True)
-    both = matmul(windows[...], wcol_hi[...], ((1,), (0,)))
-    small = matmul(windows[0:cols, :], wcol_lo[...], ((1,), (0,)))
+
+    def forward_sums():
+        for g in range(groups):
+            @pl.when(sum_slot + lats * g != d)
+            def _():
+                await_bytes(fgpart.at[g], fp_recv.at[g])
+
+        def gather_sums(i, carry):
+            send(fgpart, fgbuf.at[sum_slot], fa_send, fa_recv, lax.rem(a + i, lats), d)
+            return carry
+
+        lax.fori_loop(1, lats, gather_sums, 0)
+
+    halves = []
+    for slot in (1, 0, 2):
+        halo_arrived(back_halo, slot)
+        fill_windows(be, slot, True)
+        block = taps(slot, True)
+        halves.append(
+            (
+                matmul(windows[:, block], wcol_hi[block, :], ((1,), (0,))),
+                matmul(windows[0:cols, block], wcol_lo[block, :], ((1,), (0,))),
+            )
+        )
+        if slot == 1:
+            forward_sums()
+    both = halves[0][0] + halves[1][0] + halves[2][0]
+    small = halves[0][1] + halves[1][1] + halves[2][1]
     grad = (both[:cols] + both[cols:] + small).T
     igrad[...] = cot[...] + grad.reshape(lons, 8, cols)
+
+    exchanged(shape_send, shaped, 3)
+    out[...] = field[...] + shaped[...]
 
     await_bytes(fgbuf.at[pl.ds(0, lats - 1)], fa_recv)
     fgbuf[sum_slot] = fgpart[...]
     for i in range(lons):
         fgrad[:, i] = fgbuf[i % lats, i // lats]
-
-    exchanged(shape_send, shaped, 3)
-    out[...] = field[...] + shaped[...]
 
     for copy in field_halo + back_halo:
         copy.wait_send()
@@ -384,6 +433,18 @@
     await_bytes(fgbuf.at[pl.ds(0, lats - 1)], fa_send)
     for index, src in enumerate((cot, mixed, back_send, shape_send)):
         exchange_sent(src, index)
+
+
+def store_kernel(*refs):
+    sources, results, sems = refs[:3], refs[3:6], refs[6]
+    copies = [
+        pltpu.make_async_copy(src, dst, sems.at[i])
+        for i, (src, dst) in enumerate(zip(sources, results))
+    ]
+    for copy in copies:
+        copy.start()
+    for copy in copies:
+        copy.wait()
 
 
 def solution(mesh):
@@ -403,9 +464,13 @@
         out, igrad, fgrad = pl.pallas_call(
             functools.partial(layer_kernel, lats, lons, residues),
             out_shape=(tile, tile, jax.ShapeDtypeStruct((2,) + tiles, f32)),
-            in_specs=[vmem, vmem, pl.BlockSpec(memory_space=pl.ANY), vmem, vmem, vmem],
+            in_specs=[pl.BlockSpec(memory_space=pltpu.HBM)] * 6,
             out_specs=(vmem, vmem, vmem),
             scratch_shapes=[
+                line, line,
+                pltpu.VMEM((2,) + tiles, f32),
+                pltpu.VMEM(mats.shape, bf16),
+                pltpu.VMEM(twiddle.shape, f32),
                 pltpu.VMEM((9, chans, chans), f32),
                 pltpu.VMEM((chans, 9 * chans), bf16),
                 pltpu.VMEM((chans, 9 * chans), bf16),
@@ -424,21 +489,35 @@
                 pltpu.VMEM(share, f32),
                 pltpu.VMEM(share, f32),
                 pltpu.VMEM(shares, f32),
-                dma, dma((2, 8)), dma((2, 8)), dma((4,)), dma((4,)),
+                dma((6,)), dma((2, 8)), dma((2, 8)), dma((4,)), dma((4,)),
                 dma((groups,)), dma((groups,)), dma, dma, dma, dma,
                 dma((groups,)), dma((groups,)), dma, dma,
             ],
             compiler_params=pltpu.CompilerParams(
-                collective_id=0, has_side_effects=True, vmem_limit_bytes=48 << 20
+                collective_id=0, has_side_effects=True, vmem_limit_bytes=40 << 20
             ),
         )(
-            field.reshape(tiles),
-            cotangent.reshape(tiles),
-            conv_weight.reshape(9, chans, chans),
-            spectral_filter.reshape((2,) + tiles),
-            jnp.asarray(mats),
-            jnp.asarray(twiddle),
+            *(
+                pltpu.with_memory_space_constraint(v, pltpu.HBM)
+                for v in (
+                    field.reshape(tiles),
+                    cotangent.reshape(tiles),
+                    conv_weight.reshape(9, chans, chans),
+                    spectral_filter.reshape((2,) + tiles),
+                    jnp.asarray(mats),
+                    jnp.asarray(twiddle),
+                )
+            )
         )
+        anywhere = pl.BlockSpec(memory_space=pl.ANY)
+        out, igrad, fgrad = pl.pallas_call(
+            store_kernel,
+            out_shape=tuple(jax.ShapeDtypeStruct(v.shape, f32) for v in (out, igrad, fgrad)),
+            in_specs=[vmem] * 3,
+            out_specs=(anywhere,) * 3,
+            scratch_shapes=[dma((3,))],
+            compiler_params=pltpu.CompilerParams(has_side_effects=True),
+        )(*(pltpu.with_memory_space_constraint(v, pltpu.VMEM) for v in (out, igrad, fgrad)))
         shape = (chans, 1, cols)
         return out.reshape(shape), igrad.reshape(shape), fgrad.reshape(2, chans, cols)
 

time: 68 us -> 59.2 us (0.87)
  local copies, waits for them, and re-layouts: 8.23 us -> 0 us
    unnamed x15 -> x0, local copies, waits for them, and re-layouts: 8.23 us -> none
    pallas_call x1, Pallas kernels: 58.8 us -> 57.6 us  [on_device(): pl.pallas_call(functools.partial(layer_kernel, lats, lons, residues), out...]
    pallas_call x0 -> x1, Pallas kernels: none -> 0.82 us  [on_device(): pl.pallas_call(store_kernel, out_shape=tuple((jax.ShapeDtypeStruct(v.shap...]
where the time goes in v2:
time: 59.2 us; the launch traced here: 59.1 us
  Pallas kernels  58.4 us (99%)
  between operations  0.64 us (1%)
    pallas_call x1, Pallas kernels, on_device(): pl.pallas_call(functools.partial(layer_kernel, lats, lons, residues), out...  57.6 us

profile of v2, /device:TPU:1, one launch (start us, length us, event | category | flops | bytes accessed | tf_op | source)
XLA Modules:
  0.0 59.1 jit_solution(14317290864409760044)
XLA Ops:
  0.6 57.6 %shard_map.85 = (f32[32,8,128]{2,1,0:T(8,128)S(1)}, f32[32,8,128]{2,1,0:T(8,128)S(1)}, f32[2,32,8,128]{3,2,1,0:T(8,128)S(1)}) custom-call(f32[32,8,128]{2,1,0:T(8,128)} %bitcast.13, f32[32,8,128]{2,1,0:T(8,128)} %bitcast.14, f32[9,256,256]{2,1,0:T(8,128)} %bitcast.11, f32[2,32,8,128]{3,2,1,0:T(8,128)} %bitcast.12, ...), custom_call_target="tpu_custom_call" | custom-call | tf_op jit(solution)/shard_map/pallas_call | solution.py:464
  58.2 0.8 %shard_map.86 = (f32[32,8,128]{2,1,0:T(8,128)}, f32[32,8,128]{2,1,0:T(8,128)}, f32[2,32,8,128]{3,2,1,0:T(8,128)}) custom-call(f32[32,8,128]{2,1,0:T(8,128)S(1)} %get-tuple-element.9.refs_0_, f32[32,8,128]{2,1,0:T(8,128)S(1)} %get-tuple-element.10.refs_1_, f32[2,32,8,128]{3,2,1,0:T(8,128)S(1)} %get-tuple-element.11.refs_2_), custom_call_target="tpu_custom_call" | custom-call | tf_op jit(solution)/shard_map/pallas_call | solution.py:513

commit v3 on v2

--- a/solution.py
+++ b/solution.py
@@ -123,6 +123,41 @@
     chans = lons * 8
     ring = lons // 2
 
+    def far_first(u):
+        away = ring // 2 - (u + 2) // 4
+        away = jnp.where(lax.rem((u + 2) // 2, 2) == 1, ring - away, away)
+        half = lax.rem(d // ring + 1 - lax.rem(u, 2), 2)
+        return half * ring + lax.rem(d + away, ring)
+    up, down = lax.rem(a + 1, lats), lax.rem(a + lats - 1, lats)
+    east, west = lax.rem(d + 1, lons), lax.rem(d + lons - 1, lons)
+
+    def far_lat(v):
+        ys = lats // 4
+        u = v // 4
+        y = jnp.where(u == 0, 2, jnp.where(u == 1, 1, jnp.where(u == 2, 3, 0)))
+        x = lax.rem(a // (2 * ys) + 1 - lax.rem(v // 2, 2), 2)
+        y = lax.rem(lax.rem(a // 2, ys) + y, ys)
+        return (x * ys + y) * 2 + lax.rem(a + 1 - lax.rem(v, 2), 2)
+
+    barrier = pltpu.get_barrier_semaphore()
+
+    def greet(lat, lon):
+        pl.semaphore_signal(barrier, inc=1, device_id=(lat, lon), device_id_type=MESH)
+
+    def greet_lat(i, carry):
+        greet(lax.rem(a + i, lats), d)
+        return carry
+
+    def greet_lon(i, carry):
+        greet(a, far_first(i))
+        return carry
+
+    lax.fori_loop(0, lons - 1, greet_lon, 0)
+    lax.fori_loop(1, lats, greet_lat, 0)
+    for lat in (up, down):
+        for lon in (east, west):
+            greet(lat, lon)
+
     loads = [
         pltpu.make_async_copy(src, dst, load_sem.at[i])
         for i, (src, dst) in enumerate(
@@ -132,33 +167,6 @@
     for load in loads:
         load.start()
 
-    def far_first(u):
-        away = ring // 2 - (u + 2) // 4
-        away = jnp.where(lax.rem((u + 2) // 2, 2) == 1, ring - away, away)
-        half = lax.rem(d // ring + 1 - lax.rem(u, 2), 2)
-        return half * ring + lax.rem(d + away, ring)
-    up, down = lax.rem(a + 1, lats), lax.rem(a + lats - 1, lats)
-    east, west = lax.rem(d + 1, lons), lax.rem(d + lons - 1, lons)
-
-    barrier = pltpu.get_barrier_semaphore()
-
-    def greet(lat, lon):
-        pl.semaphore_signal(barrier, inc=1, device_id=(lat, lon), device_id_type=MESH)
-
-    def greet_lat(i, carry):
-        greet(lax.rem(a + i, lats), d)
-        return carry
-
-    def greet_lon(i, carry):
-        greet(a, far_first(i))
-        return carry
-
-    lax.fori_loop(0, lons - 1, greet_lon, 0)
-    lax.fori_loop(1, lats, greet_lat, 0)
-    for lat in (up, down):
-        for lon in (east, west):
-            greet(lat, lon)
-
     def send(src, dst, send_sem, recv_sem, lat, lon):
         copy = pltpu.make_async_remote_copy(
             src_ref=src, dst_ref=dst, send_sem=send_sem, recv_sem=recv_sem,
@@ -168,6 +176,9 @@
 
     def await_bytes(ref, sem):
         pltpu.make_async_copy(ref, ref, sem).wait()
+
+    def share_of(row):
+        return lax.rem(row + lats - lax.rem(d, lats), lats)
 
     def exchange(src, dst, index):
         def step(i, carry):
@@ -212,7 +223,7 @@
     pl.semaphore_wait(barrier, lats - 1 + lons - 1 + 4)
 
     for h in range(groups):
-        e = lax.rem(d + lats - a, lats) + lats * h
+        e = share_of(a) + lats * h
 
         @pl.when(e != d)
         def _():
@@ -259,19 +270,22 @@
         first = 2 - slot if backward else slot
         return slice(first * 3 * chans, (first * 3 + 3) * chans)
 
-    gain_slot = lax.rem(a + d, lats)
+    gain_slot = share_of(a)
+    own_share = share_of(a)
 
     def forward_gain():
-        for g in range(groups):
+        for i in range(groups):
+            g = lax.rem(d // lats + i, groups)
+
             @pl.when(gain_slot + lats * g != d)
             def _():
                 await_bytes(gpart.at[g], gp_recv.at[g])
 
-        def gather_gain(i, carry):
-            send(gpart, gbuf.at[gain_slot], ga_send, ga_recv, lax.rem(a + i, lats), d)
-            return carry
-
-        lax.fori_loop(1, lats, gather_gain, 0)
+            def gather_gain(i, carry):
+                send(gpart.at[g], gbuf.at[gain_slot, g], ga_send, ga_recv, far_lat(i), d)
+                return carry
+
+            lax.fori_loop(0, lats - 1, gather_gain, 0)
 
     halves = []
     for slot in (1, 0, 2):
@@ -341,28 +355,59 @@
     s_re, s_im = transform(mix_line)
     c_re, c_im = cspec[0], cspec[1]
     scale = 1.0 / (cols * lons)
-    tiles = (lats, groups, 8, cols)
-    pbuf[:, :, 0] = ((s_re * c_re + s_im * c_im) * scale).reshape(tiles)
-    pbuf[:, :, 1] = ((s_re * c_im - s_im * c_re) * scale).reshape(tiles)
+    for slot, r in enumerate(residues):
+        if r <= lats:
+            block = slice(slot * 8, slot * 8 + 8)
+            pbuf[r, 0] = (s_re[block] * c_re[block] + s_im[block] * c_im[block]) * scale
+            pbuf[r, 1] = (s_re[block] * c_im[block] - s_im[block] * c_re[block]) * scale
 
     def scatter_sums(i, carry):
-        peer = lax.rem(a + i, lats)
-        send(pbuf.at[lax.rem(peer + d, lats)], rsbuf.at[a], rs_send, rs_recv, peer, d)
+        peer = far_lat(i)
+        share = share_of(peer)
+        send(pbuf.at[share], rsbuf.at[0, a], rs_send.at[0], rs_recv.at[0], peer, d)
+
+        @pl.when(share == 0)
+        def _():
+            send(pbuf.at[lats], rsbuf.at[1, a], rs_send.at[1], rs_recv.at[1], peer, d)
+
         return carry
 
-    lax.fori_loop(1, lats, scatter_sums, 0)
+    lax.fori_loop(0, lats - 1, scatter_sums, 0)
 
     g_re = gbuf[:, :, 0].reshape(chans, cols)
     g_im = gbuf[:, :, 1].reshape(chans, cols)
     untransform(g_re * s_re - g_im * s_im, g_re * s_im + g_im * s_re, shape_send)
     exchange(shape_send, shaped, 3)
 
-    await_bytes(rsbuf.at[pl.ds(0, lats - 1)], rs_recv)
-    rsbuf[a] = pbuf[gain_slot]
-    fsum[...] = jnp.sum(rsbuf[...], axis=0)
-    for h in range(groups):
-        e = gain_slot + lats * h
-
+    await_bytes(rsbuf.at[0, pl.ds(0, lats - 1)], rs_recv.at[0])
+    rsbuf[0, a] = pbuf[own_share]
+    fsum[0] = jnp.sum(rsbuf[0], axis=0)
+
+    @pl.when(own_share == 0)
+    def _():
+        await_bytes(rsbuf.at[1, pl.ds(0, lats - 1)], rs_recv.at[1])
+        rsbuf[1, a] = pbuf[lats]
+        fsum[1] = jnp.sum(rsbuf[1], axis=0)
+
+    @pl.when(own_share > 0)
+    def _():
+        value = fsum[0].reshape(16, cols)
+        first, rest = split(value)
+        second, third = split(value - first.astype(f32) - rest.astype(f32))
+        place = lax.broadcasted_iota(jnp.int32, (cols, cols), 0)
+        other = lax.broadcasted_iota(jnp.int32, (cols, cols), 1)
+        mirror = jnp.where(place + other == cols - 1, 1.0, 0.0).astype(bf16)
+        parts = [matmul(part, mirror, ((1,), (0,))) for part in (first, rest, second)]
+        value = (parts[0] + parts[1] + parts[2]).reshape(2, 8, cols)
+        fsum[1, 0] = value[0]
+        fsum[1, 1] = -value[1]
+
+    def owner_of(residue):
+        width = lons.bit_length() - 1
+        return sum(lax.rem(residue // 2**bit, 2) * 2 ** (width - 1 - bit) for bit in range(width))
+
+    owners = [owner_of(own_share), owner_of(jnp.where(own_share == 0, lats, lons - own_share))]
+    for h, e in enumerate(owners):
         @pl.when(e != d)
         def _():
             send(fsum.at[h], fgpart.at[d // lats], fp_send.at[h], fp_recv.at[d // lats], a, e)
@@ -377,20 +422,25 @@
     for copy in back_halo:
         copy.start()
 
-    sum_slot = lax.rem(d + lats - a, lats)
+    residue = owner_of(d)
+    group = jnp.where(residue < lats, residue, lax.rem(lons - residue, lats))
+    sum_slot = lax.rem(a + lats - group, lats)
 
     def forward_sums():
-        for g in range(groups):
+        for i in range(groups):
+            g = lax.rem(d // lats + i, groups)
+
             @pl.when(sum_slot + lats * g != d)
             def _():
                 await_bytes(fgpart.at[g], fp_recv.at[g])
 
-        def gather_sums(i, carry):
-            send(fgpart, fgbuf.at[sum_slot], fa_send, fa_recv, lax.rem(a + i, lats), d)
-            return carry
-
-        lax.fori_loop(1, lats, gather_sums, 0)
-
+            def gather_sums(i, carry):
+                send(fgpart.at[g], fgbuf.at[sum_slot, g], fa_send, fa_recv, far_lat(i), d)
+                return carry
+
+            lax.fori_loop(0, lats - 1, gather_sums, 0)
+
+    forward_sums()
     halves = []
     for slot in (1, 0, 2):
         halo_arrived(back_halo, slot)
@@ -402,8 +452,6 @@
                 matmul(windows[0:cols, block], wcol_lo[block, :], ((1,), (0,))),
             )
         )
-        if slot == 1:
-            forward_sums()
     both = halves[0][0] + halves[1][0] + halves[2][0]
     small = halves[0][1] + halves[1][1] + halves[2][1]
     grad = (both[:cols] + both[cols:] + small).T
@@ -420,16 +468,21 @@
     for copy in field_halo + back_halo:
         copy.wait_send()
     for h in range(groups):
-        @pl.when(lax.rem(d + lats - a, lats) + lats * h != d)
+        @pl.when(share_of(a) + lats * h != d)
         def _():
             await_bytes(gpart.at[h], gp_send.at[h])
 
-        @pl.when(gain_slot + lats * h != d)
+        @pl.when(owners[h] != d)
         def _():
             await_bytes(fsum.at[h], fp_send.at[h])
 
     await_bytes(gbuf.at[pl.ds(0, lats - 1)], ga_send)
-    await_bytes(rsbuf.at[pl.ds(0, lats - 1)], rs_send)
+    await_bytes(rsbuf.at[0, pl.ds(0, lats - 1)], rs_send.at[0])
+
+    @pl.when(own_share > 0)
+    def _():
+        await_bytes(pbuf.at[lats], rs_send.at[1])
+
     await_bytes(fgbuf.at[pl.ds(0, lats - 1)], fa_send)
     for index, src in enumerate((cot, mixed, back_send, shape_send)):
         exchange_sent(src, index)
@@ -484,13 +537,13 @@
                 pltpu.VMEM((2, chans, cols), f32),
                 pltpu.VMEM(share, f32),
                 pltpu.VMEM(shares, f32),
-                pltpu.VMEM(shares, f32),
-                pltpu.VMEM(shares, f32),
+                pltpu.VMEM((lats + 1, 2, 8, cols), f32),
+                pltpu.VMEM((2, lats, 2, 8, cols), f32),
                 pltpu.VMEM(share, f32),
                 pltpu.VMEM(share, f32),
                 pltpu.VMEM(shares, f32),
                 dma((6,)), dma((2, 8)), dma((2, 8)), dma((4,)), dma((4,)),
-                dma((groups,)), dma((groups,)), dma, dma, dma, dma,
+                dma((groups,)), dma((groups,)), dma, dma, dma((2,)), dma((2,)),
                 dma((groups,)), dma((groups,)), dma, dma,
             ],
             compiler_params=pltpu.CompilerParams(

time: 59.2 us -> 56.9 us (0.961)
  Pallas kernels: 58.4 us -> 56.1 us
    pallas_call x1, Pallas kernels: 57.6 us -> 55.3 us  [on_device(): pl.pallas_call(functools.partial(layer_kernel, lats, lons, residues), out...]
where the time goes in v3:
time: 56.9 us; the launch traced here: 56.8 us
  Pallas kernels  56.1 us (99%)
  between operations  0.64 us (1%)
    pallas_call x1, Pallas kernels, on_device(): pl.pallas_call(functools.partial(layer_kernel, lats, lons, residues), out...  55.3 us

profile of v3, /device:TPU:1, one launch (start us, length us, event | category | flops | bytes accessed | tf_op | source)
XLA Modules:
  0.0 56.8 jit_solution(5251268797597868395)
XLA Ops:
  0.6 55.3 %shard_map.85 = (f32[32,8,128]{2,1,0:T(8,128)S(1)}, f32[32,8,128]{2,1,0:T(8,128)S(1)}, f32[2,32,8,128]{3,2,1,0:T(8,128)S(1)}) custom-call(f32[32,8,128]{2,1,0:T(8,128)} %bitcast.13, f32[32,8,128]{2,1,0:T(8,128)} %bitcast.14, f32[9,256,256]{2,1,0:T(8,128)} %bitcast.11, f32[2,32,8,128]{3,2,1,0:T(8,128)} %bitcast.12, ...), custom_call_target="tpu_custom_call" | custom-call | tf_op jit(solution)/shard_map/pallas_call | solution.py:517
  56.0 0.8 %shard_map.86 = (f32[32,8,128]{2,1,0:T(8,128)}, f32[32,8,128]{2,1,0:T(8,128)}, f32[2,32,8,128]{3,2,1,0:T(8,128)}) custom-call(f32[32,8,128]{2,1,0:T(8,128)S(1)} %get-tuple-element.9.refs_0_, f32[32,8,128]{2,1,0:T(8,128)S(1)} %get-tuple-element.10.refs_1_, f32[2,32,8,128]{3,2,1,0:T(8,128)S(1)} %get-tuple-element.11.refs_2_), custom_call_target="tpu_custom_call" | custom-call | tf_op jit(solution)/shard_map/pallas_call | solution.py:566

commit v4 on v3

--- a/solution.py
+++ b/solution.py
@@ -377,7 +377,6 @@
     g_re = gbuf[:, :, 0].reshape(chans, cols)
     g_im = gbuf[:, :, 1].reshape(chans, cols)
     untransform(g_re * s_re - g_im * s_im, g_re * s_im + g_im * s_re, shape_send)
-    exchange(shape_send, shaped, 3)
 
     await_bytes(rsbuf.at[0, pl.ds(0, lats - 1)], rs_recv.at[0])
     rsbuf[0, a] = pbuf[own_share]
@@ -440,6 +439,7 @@
 
             lax.fori_loop(0, lats - 1, gather_sums, 0)
 
+    exchange(shape_send, shaped, 3)
     forward_sums()
     halves = []
     for slot in (1, 0, 2):

time: 56.9 us -> 55.3 us (0.972)
  Pallas kernels: 56.1 us -> 54.3 us
    pallas_call x1, Pallas kernels: 55.3 us -> 53.5 us  [on_device(): pl.pallas_call(functools.partial(layer_kernel, lats, lons, residues), out...]
where the time goes in v4:
time: 55.3 us; the launch traced here: 55 us
  Pallas kernels  54.3 us (98%)
  between operations  0.64 us (1%)
    pallas_call x1, Pallas kernels, on_device(): pl.pallas_call(functools.partial(layer_kernel, lats, lons, residues), out...  53.5 us

profile of v4, /device:TPU:1, one launch (start us, length us, event | category | flops | bytes accessed | tf_op | source)
XLA Modules:
  0.0 55.0 jit_solution(12430893162684479469)
XLA Ops:
  0.6 53.5 %shard_map.85 = (f32[32,8,128]{2,1,0:T(8,128)S(1)}, f32[32,8,128]{2,1,0:T(8,128)S(1)}, f32[2,32,8,128]{3,2,1,0:T(8,128)S(1)}) custom-call(f32[32,8,128]{2,1,0:T(8,128)} %bitcast.13, f32[32,8,128]{2,1,0:T(8,128)} %bitcast.14, f32[9,256,256]{2,1,0:T(8,128)} %bitcast.11, f32[2,32,8,128]{3,2,1,0:T(8,128)} %bitcast.12, ...), custom_call_target="tpu_custom_call" | custom-call | tf_op jit(solution)/shard_map/pallas_call | solution.py:517
  54.2 0.8 %shard_map.86 = (f32[32,8,128]{2,1,0:T(8,128)}, f32[32,8,128]{2,1,0:T(8,128)}, f32[2,32,8,128]{3,2,1,0:T(8,128)}) custom-call(f32[32,8,128]{2,1,0:T(8,128)S(1)} %get-tuple-element.9.refs_0_, f32[32,8,128]{2,1,0:T(8,128)S(1)} %get-tuple-element.10.refs_1_, f32[2,32,8,128]{3,2,1,0:T(8,128)S(1)} %get-tuple-element.11.refs_2_), custom_call_target="tpu_custom_call" | custom-call | tf_op jit(solution)/shard_map/pallas_call | solution.py:566

commit v5 on v4

--- a/solution.py
+++ b/solution.py
@@ -101,7 +101,8 @@
     mats = []
     for mat in (forward, inverse):
         high = mat.astype(np.float32).astype(ml_dtypes.bfloat16)
-        mats += [high, (mat - high.astype(np.float64)).astype(ml_dtypes.bfloat16)]
+        low = (mat - high.astype(np.float64)).astype(ml_dtypes.bfloat16)
+        mats.append(np.concatenate([high, low, high]))
     outer = 2 * np.pi * np.outer(residues, m) / (columns * lons)
     twiddle = np.stack([np.cos(outer), np.sin(outer)]).astype(np.float32)
     return residues, np.stack(mats), twiddle
@@ -222,20 +223,20 @@
 
     pl.semaphore_wait(barrier, lats - 1 + lons - 1 + 4)
 
-    for h in range(groups):
-        e = share_of(a) + lats * h
-
-        @pl.when(e != d)
-        def _():
-            send(gain.at[:, e], gpart.at[d // lats], gp_send.at[h], gp_recv.at[d // lats], a, e)
-
-        @pl.when(e == d)
-        def _():
-            gpart[d // lats] = gain[:, e]
-
     field_halo = halo_plan(xe, 0)
     for copy in field_halo:
         copy.start()
+
+    for h in range(groups):
+        e = share_of(a) + lats * h
+
+        @pl.when(e != d)
+        def _():
+            send(gain.at[:, e], gpart.at[d // lats], gp_send.at[h], gp_recv.at[d // lats], a, e)
+
+        @pl.when(e == d)
+        def _():
+            gpart[d // lats] = gain[:, e]
 
     exchange(cot, cot_line, 0)
 
@@ -317,14 +318,12 @@
                 lhs[block, 0:cols] = re * c + im * s
                 lhs[block, cols : 2 * cols] = im * c - re * s
         hi, lo = split(lhs[...])
-        dims = ((1,), (0,))
-        full = matmul(hi, mats[0], dims) + matmul(hi, mats[1], dims) + matmul(lo, mats[0], dims)
+        full = matmul(jnp.concatenate([hi, hi, lo], axis=1), mats[0], ((1,), (0,)))
         return full[:, :cols], full[:, cols:]
 
     def untransform(re, im, dst):
         hi, lo = split(jnp.concatenate([re, im], axis=1))
-        dims = ((1,), (0,))
-        lhs[...] = matmul(hi, mats[2], dims) + matmul(hi, mats[3], dims) + matmul(lo, mats[2], dims)
+        lhs[...] = matmul(jnp.concatenate([hi, hi, lo], axis=1), mats[1], ((1,), (0,)))
         turned = [None] * lons
         for slot, r in enumerate(residues):
             block = slice(slot * 8, slot * 8 + 8)
@@ -382,6 +381,24 @@
     rsbuf[0, a] = pbuf[own_share]
     fsum[0] = jnp.sum(rsbuf[0], axis=0)
 
+    def owner_of(residue):
+        width = lons.bit_length() - 1
+        return sum(lax.rem(residue // 2**bit, 2) * 2 ** (width - 1 - bit) for bit in range(width))
+
+    owners = [owner_of(own_share), owner_of(jnp.where(own_share == 0, lats, lons - own_share))]
+    def pass_on(h):
+        e = owners[h]
+
+        @pl.when(e != d)
+        def _():
+            send(fsum.at[h], fgpart.at[d // lats], fp_send.at[h], fp_recv.at[d // lats], a, e)
+
+        @pl.when(e == d)
+        def _():
+            fgpart[d // lats] = fsum[h]
+
+    pass_on(0)
+
     @pl.when(own_share == 0)
     def _():
         await_bytes(rsbuf.at[1, pl.ds(0, lats - 1)], rs_recv.at[1])
@@ -401,19 +418,7 @@
         fsum[1, 0] = value[0]
         fsum[1, 1] = -value[1]
 
-    def owner_of(residue):
-        width = lons.bit_length() - 1
-        return sum(lax.rem(residue // 2**bit, 2) * 2 ** (width - 1 - bit) for bit in range(width))
-
-    owners = [owner_of(own_share), owner_of(jnp.where(own_share == 0, lats, lons - own_share))]
-    for h, e in enumerate(owners):
-        @pl.when(e != d)
-        def _():
-            send(fsum.at[h], fgpart.at[d // lats], fp_send.at[h], fp_recv.at[d // lats], a, e)
-
-        @pl.when(e == d)
-        def _():
-            fgpart[d // lats] = fsum[h]
+    pass_on(1)
 
     exchanged(back_send, back, 2)
     be[1, middle] = back[...].reshape(chans, cols).T

time: 55.3 us -> 55.2 us (level)
  no operation moved by 1% of the time
where the time goes in v5:
time: 55.2 us; the launch traced here: 55.1 us
  Pallas kernels  54.5 us (99%)
  between operations  0.64 us (1%)
    pallas_call x1, Pallas kernels, on_device(): pl.pallas_call(functools.partial(layer_kernel, lats, lons, residues), out...  53.6 us

profile of v5, /device:TPU:1, one launch (start us, length us, event | category | flops | bytes accessed | tf_op | source)
XLA Modules:
  0.0 55.1 jit_solution(1360883786462686210)
XLA Ops:
  0.6 53.6 %shard_map.85 = (f32[32,8,128]{2,1,0:T(8,128)S(1)}, f32[32,8,128]{2,1,0:T(8,128)S(1)}, f32[2,32,8,128]{3,2,1,0:T(8,128)S(1)}) custom-call(f32[32,8,128]{2,1,0:T(8,128)} %bitcast.13, f32[32,8,128]{2,1,0:T(8,128)} %bitcast.14, f32[9,256,256]{2,1,0:T(8,128)} %bitcast.11, f32[2,32,8,128]{3,2,1,0:T(8,128)} %bitcast.12, ...), custom_call_target="tpu_custom_call" | custom-call | tf_op jit(solution)/shard_map/pallas_call | solution.py:522
  54.3 0.8 %shard_map.86 = (f32[32,8,128]{2,1,0:T(8,128)}, f32[32,8,128]{2,1,0:T(8,128)}, f32[2,32,8,128]{3,2,1,0:T(8,128)}) custom-call(f32[32,8,128]{2,1,0:T(8,128)S(1)} %get-tuple-element.9.refs_0_, f32[32,8,128]{2,1,0:T(8,128)S(1)} %get-tuple-element.10.refs_1_, f32[2,32,8,128]{3,2,1,0:T(8,128)S(1)} %get-tuple-element.11.refs_2_), custom_call_target="tpu_custom_call" | custom-call | tf_op jit(solution)/shard_map/pallas_call | solution.py:571
